TPU v7x, 768 devices: a whole 4x8x12 slice. The times are simulated.
768 devices in a mesh: grp: 48 (over z, x), sub: 16 (over y, core).
Axes of the slice: x: 4, y: 8, z: 12, core: 2. Of those that a mesh axis runs over, the one named last changes fastest.
Arguments:
- load: float32 [48, 16, 15, 384], P('grp', 'sub'), may hold values from -6 to 6
- couple: bfloat16 [48, 16, 4, 15, 15, 384], P('grp', 'sub'), may hold values from -1 to 6
- face_link: int32 [48, 16, 3, 384], P('grp', 'sub'), may hold values from 0 to 383, as said below
- face_count: int32 [48, 16], P('grp', 'sub'), may hold values from 256 to 384, as said below
- slot_face: int32 [48, 16, 16, 32], P('grp', 'sub'), may hold values from 0 to 383, as said below
- pair_count: int32 [48, 16, 16], P('grp', 'sub'), may hold values from 0 to 32, as said below
- basis: float32 [48, 16, 64, 15, 384], P('grp', 'sub'), may hold values from -0.0390625 to 0.0390625
- coarse_inverse: float32 [48, 16, 64, 64], P('grp', 'sub'), may hold values from -0.25 to 1.65
- coarse_block: float32 [48, 16, 6, 64, 64], P('grp', 'sub'), may hold values from -0.15625 to 0.15625
- coarse_link: int32 [48, 16, 6], P('grp', 'sub'), may hold values from 0 to 767, as said below
Outputs:
- trace_field: float32 [48, 16, 15, 384], P('grp', 'sub')
- robin_data: float32 [48, 16, 15, 384], P('grp', 'sub')
- coarse_coef: float32 [48, 16, 64], P('grp', 'sub')
Inputs may be any that keep to these rules, and one draw needn't show every extreme that they name: Subdomain (g, i) has live face blocks 0 to face_count[g, i] - 1; the rest are padding. Some subdomain has all 384 live. pair_count[g, i, j] equals pair_count[g, j, i], is 0 for j = i and otherwise 1 or more, a quarter of 32 or more, rounded down; every subdomain has exactly one peer with 32, and all its other peers have half of 32 or fewer. `slot_face`: for c < pair_count[g, i, j], slot c toward j names a live face block of i that i shares with j, the same face that slot c of j toward i names on j's side; these faces are distinct within a subdomain. Other slots name any face block. `face_link`: linked face blocks are live and differ from the face block itself. `coarse_link`: the 6 coarse neighbours of subdomain (g, i) are distinct, differ from it, and lie in groups g - 1, g or g + 1.
All inputs are finite; a program needn't handle non-finite values.
Results may differ from a plain program's by a relative error of at most 0.0015.
Values sent between devices are 32-bit elements; how exact they have to be, the bound alone decides.
No kernel may reach another device: no remote copies, remote signals or barrier semaphores. Data moves between devices by JAX's collectives and lax.ppermute only.
A program may use at most 32 MiB of HBM per device.

v0:
```python
import jax
import jax.numpy as jnp
from jax import lax
from jax.sharding import PartitionSpec as P

FB = 384
CAP = 32
ITERS = 3
SWEEPS = 2
CSWEEPS = 2


robin_weight = 1.0
omega_step = 0.2
highest = lax.Precision.HIGHEST


def extended(shard, sides, width):
    for axis, dim in sides:
        size, length = (lax.axis_size(axis), shard.shape[dim])
        up = [(i, (i + 1) % size) for i in range(size - 1)]
        down = [(j, i) for i, j in up]
        last = lax.slice_in_dim(shard, length - width, length, axis=dim)
        first = lax.slice_in_dim(shard, 0, width, axis=dim)
        before = lax.ppermute(last, axis, up)
        after = lax.ppermute(first, axis, down)
        shard = jnp.concatenate([before, shard, after], axis=dim)
    return shard


def couple_apply(couple, face_links, trace_rows, live_mask, interface):
    linked = jnp.moveaxis(trace_rows[:, face_links], 1, 0)
    stacked = jnp.concatenate([trace_rows[None], linked], axis=0)
    product = jnp.sum(couple * stacked[:, None, :, :], axis=(0, 2))
    return live_mask * (product + robin_weight * interface * trace_rows)


def masks_for(own_count, own_slots, own_pairs):
    live_mask = (jnp.arange(FB) < own_count).astype(jnp.float32)
    valid_slots = jnp.arange(CAP)[None, :] < own_pairs[:, None]
    counted = jnp.zeros((FB,), jnp.float32).at[own_slots].add(valid_slots.astype(jnp.float32))
    return (live_mask, jnp.minimum(counted, 1.0), valid_slots)


def local_phase(
    load_rows, couple, face_links, live_mask, interface, basis_rows, trace_field, robin_data
):
    for sweep_index in range(SWEEPS):
        residual = live_mask * (load_rows + robin_data) - couple_apply(
            couple, face_links, trace_field, live_mask, interface
        )
        trace_field = trace_field + omega_step * residual
    residual = live_mask * (load_rows + robin_data) - couple_apply(
        couple, face_links, trace_field, live_mask, interface
    )
    restricted = jnp.dot(
        basis_rows.reshape(basis_rows.shape[0], -1), residual.reshape(-1), precision=highest
    )
    return (trace_field, restricted)


def neighbours(coefficients, neighbour_ids):
    group_index = lax.axis_index("grp")
    peer_count = lax.axis_size("sub")
    members = lax.all_gather(coefficients[None], "sub", axis=0, tiled=True)
    band_rows = extended(members[None], (("grp", 0),), 1)
    stacked_rows = band_rows.reshape(3 * peer_count, -1)
    positions = neighbour_ids - (group_index - 1) * peer_count
    return stacked_rows[positions]


def body(
    load,
    couple,
    face_link,
    face_count,
    slot_face,
    pair_count,
    basis,
    coarse_inverse,
    coarse_block,
    coarse_link,
):
    load_rows = load[0, 0]
    couple_rows = couple[0, 0]
    face_links = face_link[0, 0]
    own_slots = slot_face[0, 0]
    basis_rows = basis[0, 0]
    inverse_block = coarse_inverse[0, 0]
    coupling = coarse_block[0, 0]
    neighbour_ids = coarse_link[0, 0]
    live_mask, interface, valid_slots = masks_for(face_count[0, 0], own_slots, pair_count[0, 0])
    basis_flat = basis_rows.reshape(basis_rows.shape[0], -1)
    own_index = lax.axis_index("sub")
    trace_field = jnp.zeros(load_rows.shape, jnp.float32)
    robin_data = jnp.zeros(load_rows.shape, jnp.float32)
    coefficients = jnp.zeros((basis_rows.shape[0],), jnp.float32)
    for outer_step in range(ITERS):
        trace_field, restricted = local_phase(
            load_rows,
            couple_rows,
            face_links,
            live_mask,
            interface,
            basis_rows,
            trace_field,
            robin_data,
        )
        coarse_start = jnp.dot(inverse_block, restricted, precision=highest)
        coefficients = coarse_start
        for inner_step in range(CSWEEPS):
            gathered = neighbours(coefficients, neighbour_ids)
            coupled = jnp.einsum("kvw,kw->v", coupling, gathered, precision=highest)
            coefficients = coarse_start - jnp.dot(inverse_block, coupled, precision=highest)
        correction = jnp.dot(coefficients, basis_flat, precision=highest).reshape(trace_field.shape)
        trace_field = trace_field + live_mask * correction
        outgoing = (2.0 * robin_weight * trace_field - robin_data)[:, own_slots]
        own_part = lax.dynamic_index_in_dim(
            lax.all_gather(outgoing[None], "sub", axis=0, tiled=True), own_index, 2, keepdims=False
        )
        received = jnp.swapaxes(own_part, 0, 1)
        received = jnp.where(valid_slots[None], received, 0.0)
        robin_data = jnp.zeros(load_rows.shape, jnp.float32).at[:, own_slots].add(received)
    return (trace_field[None, None], robin_data[None, None], coefficients[None, None])


def solution(mesh):
    in_specs = (
        P("grp", "sub", None, None),
        P("grp", "sub", None, None, None, None),
        P("grp", "sub", None, None),
        P("grp", "sub"),
        P("grp", "sub", None, None),
        P("grp", "sub", None),
        P("grp", "sub", None, None, None),
        P("grp", "sub", None, None),
        P("grp", "sub", None, None, None),
        P("grp", "sub", None),
    )
    out_specs = (P("grp", "sub", None, None), P("grp", "sub", None, None), P("grp", "sub", None))
    return jax.shard_map(body, mesh=mesh, in_specs=in_specs, out_specs=out_specs, check_vma=False)
```

profile of v0, /device:TPU:513, one launch (start us, length us, event | category | flops | bytes accessed | tf_op | source)
XLA Modules:
  0.0 352.0 jit_solution(8819463177561390029)
XLA Ops:
  2.3 2.4 gather_fusion
  5.2 4.1 %scatter_custom_fusion = f32[384]{0:T(512)S(1)} fusion(s32[512]{0:T(512)S(1)} %reshape.580, f32[512]{0:T(512)S(1)} %reshape.582, f32[]{:T(128)} %constant.12.clone.1), kind=kCustom, calls=%fused_computation.170 | custom fusion | flops 512 | bytes 1540 | tf_op jit(solution)/shard_map/scatter-add | solution.py:41
  10.6 2.4 gather_fusion.1
  14.0 2.4 gather_fusion.2
  17.4 1.1 copy-done.3
  18.5 1.3 convolution_bitcast_fusion.2
  20.0 1.3 dynamic-slice
  22.2 24.2 %all-reduce.1 = f32[1024]{0:T(1024)S(1)} all-reduce(f32[1024]{0:T(1024)S(1)} %dynamic-update-slice), channel_id=2, replica_groups=mesh['grp'=48,'sub'=16] {'sub'}, use_global_device_ids=true, to_apply=%add.1 | all-reduce | flops 1024 | bytes 8192
  46.4 5.6 %collective-permute-start.1 = (f32[1,16,64]{2,1,0:T(8,128)S(1)}, f32[1,16,64]{2,1,0:T(8,128)S(1)}, u32[]{:S(2)}, u32[]{:S(2)}) collective-permute-start(f32[1,16,64]{2,1,0:T(8,128)S(1)} %broadcast_in_dim.72), channel_id=1, source_target_pairs={{16,0},{32,16},{48,32},{64,48},{80,64},{96,80},{112,96},{128,112},... | collective-permute-start | bytes 12296 | tf_op jit(solution)/shard_map/ppermute | solution.py:26
  52.0 1.9 collective-permute-start
  54.0 5.7 %collective-permute-done = f32[1,16,64]{2,1,0:T(8,128)S(1)} collective-permute-done((f32[1,16,64]{2,1,0:T(8,128)S(1)}, f32[1,16,64]{2,1,0:T(8,128)S(1)}, u32[]{:S(2)}, u32[]{:S(2)}) %collective-permute-start) | collective-permute-done | bytes 4128 | tf_op jit(solution)/shard_map/ppermute | solution.py:25
  61.0 27.2 %all-reduce.2 = f32[1024]{0:T(1024)S(1)} all-reduce(f32[1024]{0:T(1024)S(1)} %dynamic-update-slice.1), channel_id=3, replica_groups=mesh['grp'=48,'sub'=16] {'sub'}, use_global_device_ids=true, to_apply=%add.2 | all-reduce | flops 1024 | bytes 8192
  88.3 1.9 collective-permute-start.3
  90.2 3.4 collective-permute-start.2
  93.6 4.3 %collective-permute-done.2 = f32[1,16,64]{2,1,0:T(8,128)S(1)} collective-permute-done((f32[1,16,64]{2,1,0:T(8,128)S(1)}, f32[1,16,64]{2,1,0:T(8,128)S(1)}, u32[]{:S(2)}, u32[]{:S(2)}) %collective-permute-start.2) | collective-permute-done | bytes 4128 | tf_op jit(solution)/shard_map/ppermute | solution.py:25
  99.9 1.0 gather_fusion.5
  101.1 23.6 %all-gather.2 = f32[240,16,32]{2,1,0:T(8,128)S(1)} all-gather(f32[15,16,32]{2,1,0:T(8,128)S(1)} %bitcast.360), channel_id=4, replica_groups=mesh['grp'=48,'sub'=16] {'sub'}, dimensions={0}, use_global_device_ids=true | all-gather | bytes 522240 | tf_op jit(solution)/shard_map/all_gather | solution.py:119
  125.0 2.5 scatter_custom_fusion.1
  127.8 2.4 gather_fusion.6
  131.2 2.4 gather_fusion.7
  134.5 2.4 gather_fusion.8
  137.8 2.6 convolution_bitcast_fusion.1
  140.8 23.0 %all-reduce.3 = f32[1024]{0:T(1024)S(1)} all-reduce(f32[1024]{0:T(1024)S(1)} %dynamic-update-slice.2), channel_id=5, replica_groups=mesh['grp'=48,'sub'=16] {'sub'}, use_global_device_ids=true, to_apply=%add.3 | all-reduce | flops 1024 | bytes 8192
  163.9 1.9 collective-permute-start.5
  165.9 3.4 collective-permute-start.4
  169.2 4.3 %collective-permute-done.4 = f32[1,16,64]{2,1,0:T(8,128)S(1)} collective-permute-done((f32[1,16,64]{2,1,0:T(8,128)S(1)}, f32[1,16,64]{2,1,0:T(8,128)S(1)}, u32[]{:S(2)}, u32[]{:S(2)}) %collective-permute-start.4) | collective-permute-done | bytes 4128 | tf_op jit(solution)/shard_map/ppermute | solution.py:25
  174.8 25.0 %all-reduce.4 = f32[1024]{0:T(1024)S(1)} all-reduce(f32[1024]{0:T(1024)S(1)} %dynamic-update-slice.3), channel_id=6, replica_groups=mesh['grp'=48,'sub'=16] {'sub'}, use_global_device_ids=true, to_apply=%add.4 | all-reduce | flops 1024 | bytes 8192
  199.9 1.9 collective-permute-start.7
  201.8 3.4 collective-permute-start.6
  205.2 4.3 %collective-permute-done.6 = f32[1,16,64]{2,1,0:T(8,128)S(1)} collective-permute-done((f32[1,16,64]{2,1,0:T(8,128)S(1)}, f32[1,16,64]{2,1,0:T(8,128)S(1)}, u32[]{:S(2)}, u32[]{:S(2)}) %collective-permute-start.6) | collective-permute-done | bytes 4128 | tf_op jit(solution)/shard_map/ppermute | solution.py:25
  211.5 1.0 gather_fusion.11
  212.7 23.6 %all-gather.5 = f32[240,16,32]{2,1,0:T(8,128)S(1)} all-gather(f32[15,16,32]{2,1,0:T(8,128)S(1)} %bitcast.361), channel_id=7, replica_groups=mesh['grp'=48,'sub'=16] {'sub'}, dimensions={0}, use_global_device_ids=true | all-gather | bytes 522240 | tf_op jit(solution)/shard_map/all_gather | solution.py:119
  236.7 2.5 scatter_custom_fusion.2
  239.4 2.4 gather_fusion.12
  242.8 2.4 gather_fusion.13
  246.2 2.4 gather_fusion.14
  249.5 2.6 convolution_bitcast_fusion
  252.5 23.0 %all-reduce.5 = f32[1024]{0:T(1024)S(1)} all-reduce(f32[1024]{0:T(1024)S(1)} %dynamic-update-slice.4), channel_id=8, replica_groups=mesh['grp'=48,'sub'=16] {'sub'}, use_global_device_ids=true, to_apply=%add.5 | all-reduce | flops 1024 | bytes 8192
  275.6 1.9 collective-permute-start.9
  277.5 3.4 collective-permute-start.8
  280.9 4.3 %collective-permute-done.8 = f32[1,16,64]{2,1,0:T(8,128)S(1)} collective-permute-done((f32[1,16,64]{2,1,0:T(8,128)S(1)}, f32[1,16,64]{2,1,0:T(8,128)S(1)}, u32[]{:S(2)}, u32[]{:S(2)}) %collective-permute-start.8) | collective-permute-done | bytes 4128 | tf_op jit(solution)/shard_map/ppermute | solution.py:25
  286.5 25.0 %all-reduce.6 = f32[1024]{0:T(1024)S(1)} all-reduce(f32[1024]{0:T(1024)S(1)} %dynamic-update-slice.5), channel_id=9, replica_groups=mesh['grp'=48,'sub'=16] {'sub'}, use_global_device_ids=true, to_apply=%add.6 | all-reduce | flops 1024 | bytes 8192
  311.6 1.9 collective-permute-start.11
  313.5 3.4 collective-permute-start.10
  316.9 4.3 %collective-permute-done.10 = f32[1,16,64]{2,1,0:T(8,128)S(1)} collective-permute-done((f32[1,16,64]{2,1,0:T(8,128)S(1)}, f32[1,16,64]{2,1,0:T(8,128)S(1)}, u32[]{:S(2)}, u32[]{:S(2)}) %collective-permute-start.10) | collective-permute-done | bytes 4128 | tf_op jit(solution)/shard_map/ppermute | solution.py:25
  323.8 1.0 gather_fusion.17
  325.1 23.6 %all-gather.8 = f32[240,16,32]{2,1,0:T(8,128)S(1)} all-gather(f32[15,16,32]{2,1,0:T(8,128)S(1)} %bitcast.362), channel_id=10, replica_groups=mesh['grp'=48,'sub'=16] {'sub'}, dimensions={0}, use_global_device_ids=true | all-gather | bytes 522240 | tf_op jit(solution)/shard_map/all_gather | solution.py:119
  349.0 2.3 scatter_custom_fusion.3
  (164 shorter events, 23.9 us)
Async XLA Ops:
  0.6 59.7 %copy-start = (f32[1,1,6,64,64]{4,3,2,1,0:T(8,128)S(1)}, f32[1,1,6,64,64]{4,3,2,1,0:T(8,128)}, u32[]{:S(2)}) copy-start(f32[1,1,6,64,64]{4,3,2,1,0:T(8,128)} %param.18) | copy-start | bytes 294916
  0.6 4.4 %copy-start.7 = (s32[1,1,16]{2,1,0:T(1,128)S(1)}, s32[1,1,16]{2,1,0:T(1,128)}, u32[]{:S(2)}) copy-start(s32[1,1,16]{2,1,0:T(1,128)} %param.15) | copy-start | bytes 196
  0.7 9.3 %copy-start.1 = (bf16[1,1,4,15,15,384]{5,2,4,3,1,0:T(4,128)(2,1)S(1)}, bf16[1,1,4,15,15,384]{5,2,4,3,1,0:T(4,128)(2,1)}, u32[]{:S(2)}) copy-start(bf16[1,1,4,15,15,384]{5,2,4,3,1,0:T(4,128)(2,1)} %param.11) | copy-start | bytes 2073604
  0.7 9.7 %copy-start.4 = (f32[1,1,15,384]{3,1,2,0:T(1,128)S(1)}, f32[1,1,15,384]{3,1,2,0:T(1,128)}, u32[]{:S(2)}) copy-start(f32[1,1,15,384]{3,1,2,0:T(1,128)} %param.10) | copy-start | bytes 69124
  13.9 3.4 copy-start.2
  17.4 1.1 copy-start.3
  17.4 2.4 copy-start.5
  17.4 36.5 %copy-start.8 = (s32[1,1,6]{2,1,0:T(1,128)S(1)}, s32[1,1,6]{2,1,0:T(1,128)}, u32[]{:S(2)}) copy-start(s32[1,1,6]{2,1,0:T(1,128)} %param.19) | copy-start | bytes 76
  46.4 7.6 %collective-permute-start.1 = (f32[1,16,64]{2,1,0:T(8,128)S(1)}, f32[1,16,64]{2,1,0:T(8,128)S(1)}, u32[]{:S(2)}, u32[]{:S(2)}) collective-permute-start(f32[1,16,64]{2,1,0:T(8,128)S(1)} %broadcast_in_dim.72), channel_id=1, source_target_pairs={{16,0},{32,16},{48,32},{64,48},{80,64},{96,80},{112,96},{128,112},... | collective-permute-start | bytes 12296 | tf_op jit(solution)/shard_map/ppermute | solution.py:26
  52.0 7.7 %collective-permute-start = (f32[1,16,64]{2,1,0:T(8,128)S(1)}, f32[1,16,64]{2,1,0:T(8,128)S(1)}, u32[]{:S(2)}, u32[]{:S(2)}) collective-permute-start(f32[1,16,64]{2,1,0:T(8,128)S(1)} %broadcast_in_dim.72), channel_id=1, source_target_pairs={{0,16},{16,32},{32,48},{48,64},{64,80},{80,96},{96,112},{112,128},... | collective-permute-start | bytes 12296 | tf_op jit(solution)/shard_map/ppermute | solution.py:25
  88.3 5.3 %collective-permute-start.3 = (f32[1,16,64]{2,1,0:T(8,128)S(1)}, f32[1,16,64]{2,1,0:T(8,128)S(1)}, u32[]{:S(2)}, u32[]{:S(2)}) collective-permute-start(f32[1,16,64]{2,1,0:T(8,128)S(1)} %broadcast_in_dim.74), channel_id=1, source_target_pairs={{16,0},{32,16},{48,32},{64,48},{80,64},{96,80},{112,96},{128,112},... | collective-permute-start | bytes 12296 | tf_op jit(solution)/shard_map/ppermute | solution.py:26
  90.2 7.7 %collective-permute-start.2 = (f32[1,16,64]{2,1,0:T(8,128)S(1)}, f32[1,16,64]{2,1,0:T(8,128)S(1)}, u32[]{:S(2)}, u32[]{:S(2)}) collective-permute-start(f32[1,16,64]{2,1,0:T(8,128)S(1)} %broadcast_in_dim.74), channel_id=1, source_target_pairs={{0,16},{16,32},{32,48},{48,64},{64,80},{80,96},{96,112},{112,128},... | collective-permute-start | bytes 12296 | tf_op jit(solution)/shard_map/ppermute | solution.py:25
  163.9 5.3 %collective-permute-start.5 = (f32[1,16,64]{2,1,0:T(8,128)S(1)}, f32[1,16,64]{2,1,0:T(8,128)S(1)}, u32[]{:S(2)}, u32[]{:S(2)}) collective-permute-start(f32[1,16,64]{2,1,0:T(8,128)S(1)} %broadcast_in_dim.82), channel_id=1, source_target_pairs={{16,0},{32,16},{48,32},{64,48},{80,64},{96,80},{112,96},{128,112},... | collective-permute-start | bytes 12296 | tf_op jit(solution)/shard_map/ppermute | solution.py:26
  165.9 7.7 %collective-permute-start.4 = (f32[1,16,64]{2,1,0:T(8,128)S(1)}, f32[1,16,64]{2,1,0:T(8,128)S(1)}, u32[]{:S(2)}, u32[]{:S(2)}) collective-permute-start(f32[1,16,64]{2,1,0:T(8,128)S(1)} %broadcast_in_dim.82), channel_id=1, source_target_pairs={{0,16},{16,32},{32,48},{48,64},{64,80},{80,96},{96,112},{112,128},... | collective-permute-start | bytes 12296 | tf_op jit(solution)/shard_map/ppermute | solution.py:25
  199.9 5.3 %collective-permute-start.7 = (f32[1,16,64]{2,1,0:T(8,128)S(1)}, f32[1,16,64]{2,1,0:T(8,128)S(1)}, u32[]{:S(2)}, u32[]{:S(2)}) collective-permute-start(f32[1,16,64]{2,1,0:T(8,128)S(1)} %broadcast_in_dim.84), channel_id=1, source_target_pairs={{16,0},{32,16},{48,32},{64,48},{80,64},{96,80},{112,96},{128,112},... | collective-permute-start | bytes 12296 | tf_op jit(solution)/shard_map/ppermute | solution.py:26
  201.8 7.7 %collective-permute-start.6 = (f32[1,16,64]{2,1,0:T(8,128)S(1)}, f32[1,16,64]{2,1,0:T(8,128)S(1)}, u32[]{:S(2)}, u32[]{:S(2)}) collective-permute-start(f32[1,16,64]{2,1,0:T(8,128)S(1)} %broadcast_in_dim.84), channel_id=1, source_target_pairs={{0,16},{16,32},{32,48},{48,64},{64,80},{80,96},{96,112},{112,128},... | collective-permute-start | bytes 12296 | tf_op jit(solution)/shard_map/ppermute | solution.py:25
  275.6 5.3 %collective-permute-start.9 = (f32[1,16,64]{2,1,0:T(8,128)S(1)}, f32[1,16,64]{2,1,0:T(8,128)S(1)}, u32[]{:S(2)}, u32[]{:S(2)}) collective-permute-start(f32[1,16,64]{2,1,0:T(8,128)S(1)} %broadcast_in_dim.90), channel_id=1, source_target_pairs={{16,0},{32,16},{48,32},{64,48},{80,64},{96,80},{112,96},{128,112},... | collective-permute-start | bytes 12296 | tf_op jit(solution)/shard_map/ppermute | solution.py:26
  277.5 7.7 %collective-permute-start.8 = (f32[1,16,64]{2,1,0:T(8,128)S(1)}, f32[1,16,64]{2,1,0:T(8,128)S(1)}, u32[]{:S(2)}, u32[]{:S(2)}) collective-permute-start(f32[1,16,64]{2,1,0:T(8,128)S(1)} %broadcast_in_dim.90), channel_id=1, source_target_pairs={{0,16},{16,32},{32,48},{48,64},{64,80},{80,96},{96,112},{112,128},... | collective-permute-start | bytes 12296 | tf_op jit(solution)/shard_map/ppermute | solution.py:25
  311.6 5.3 %collective-permute-start.11 = (f32[1,16,64]{2,1,0:T(8,128)S(1)}, f32[1,16,64]{2,1,0:T(8,128)S(1)}, u32[]{:S(2)}, u32[]{:S(2)}) collective-permute-start(f32[1,16,64]{2,1,0:T(8,128)S(1)} %broadcast_in_dim.92), channel_id=1, source_target_pairs={{16,0},{32,16},{48,32},{64,48},{80,64},{96,80},{112,96},{128,112},... | collective-permute-start | bytes 12296 | tf_op jit(solution)/shard_map/ppermute | solution.py:26
  313.5 7.7 %collective-permute-start.10 = (f32[1,16,64]{2,1,0:T(8,128)S(1)}, f32[1,16,64]{2,1,0:T(8,128)S(1)}, u32[]{:S(2)}, u32[]{:S(2)}) collective-permute-start(f32[1,16,64]{2,1,0:T(8,128)S(1)} %broadcast_in_dim.92), channel_id=1, source_target_pairs={{0,16},{16,32},{32,48},{48,64},{64,80},{80,96},{96,112},{112,128},... | collective-permute-start | bytes 12296 | tf_op jit(solution)/shard_map/ppermute | solution.py:25
  322.2 2.7 copy-start.6
where the time goes:
time: 353 us; the launch traced here: 352 us
  blocking collectives  218 us (62%)
  local copies, waits for them, and re-layouts  40.1 us (11%)
  starting transfers between devices  33.9 us (10%)
  waiting for transfers between devices  27.4 us (8%)
  other arithmetic  17.2 us (5%)
  matrix products  12 us (3%)
    unnamed x6, blocking collectives  148 us
    all_gather x3, blocking collectives, body(): lax.all_gather(outgoing[None], 'sub', axis=0, tiled=True)  70.9 us
    ppermute x6, waiting for transfers between devices, extended(): before = lax.ppermute(last, axis, up)  27.4 us
    gather x17, local copies, waits for them, and re-layouts, couple_apply(): linked = jnp.moveaxis(trace_rows[:, face_links], 1, 0)  24.1 us
    ppermute x6, starting transfers between devices, extended(): before = lax.ppermute(last, axis, up)  18.7 us
    ppermute x6, starting transfers between devices, extended(): after = lax.ppermute(first, axis, down)  15.1 us
    scatter-add x3, other arithmetic, body(): jnp.zeros(load_rows.shape, jnp.float32).at[:, own_slots].add(received)  7.29 us
  transfers between devices with their start and end apart: 12, of which 6 were waited for; matrix products, arithmetic and copies ran while one was open for 0% of the time, Pallas kernels for 0%

commit v1 on v0

v1 whole, which is shorter than its diff:
```python
import functools

import jax
import jax.numpy as jnp
from jax import lax
from jax.experimental import pallas as pl
from jax.experimental.pallas import tpu as pltpu
from jax.sharding import PartitionSpec as P

TRACE = 15
ROWS = 16
FB = 384
CAP = 32
LANES = 128
LINKS = 3
CVEC = 64
KC = 6
ITERS = 3
SWEEPS = 2

robin_weight = 1.0
omega_step = 0.2
f32 = jnp.float32


def pick(pieces, index):
    low = jnp.bitwise_and(index, LANES - 1)
    high = jnp.right_shift(index, 7)
    out = None
    for at, piece in enumerate(pieces):
        taken = jnp.take_along_axis(piece, low, axis=1, mode="promise_in_bounds")
        out = taken if out is None else jnp.where(high == at, taken, out)
    return out


def tiles_of(rows):
    return [rows[:, t * LANES : (t + 1) * LANES] for t in range(rows.shape[1] // LANES)]


def pick_faces(rows, index_row):
    pieces = tiles_of(rows)
    picked = [
        pick(pieces, jnp.broadcast_to(part, (rows.shape[0], LANES))) for part in tiles_of(index_row)
    ]
    return jnp.concatenate(picked, axis=1)


def live_row(count):
    return (lax.broadcasted_iota(jnp.int32, (1, FB), 1) < count).astype(f32)


def eye(offset):
    row = lax.broadcasted_iota(jnp.int32, (CVEC, LANES), 0)
    lane = lax.broadcasted_iota(jnp.int32, (CVEC, LANES), 1)
    return lane == row + offset


def matvec(matrix, row):
    return jnp.sum(matrix * row, axis=1, keepdims=True)


def as_row(low, high):
    spread = jnp.where(eye(0), low, 0.0) + jnp.where(eye(CVEC), high, 0.0)
    return jnp.sum(spread, axis=0, keepdims=True)


def couple_apply(couple_ref, link_ref, trace, live, interface, sum_ref):
    stacked = [trace] + [pick_faces(trace, link_ref[k : k + 1, :]) for k in range(LINKS)]
    stacked = [rows[:TRACE] for rows in stacked]
    for a in range(TRACE):
        product = stacked[0] * couple_ref[0, a].astype(f32)
        for k in range(1, LINKS + 1):
            product = product + stacked[k] * couple_ref[k, a].astype(f32)
        sum_ref[a : a + 1, :] = jnp.sum(product, axis=0, keepdims=True)
    return live * (sum_ref[...] + robin_weight * interface * trace)


def unpack_slots(arrived_ref, inverse_row):
    lane = lax.broadcasted_iota(jnp.int32, (8, LANES), 1) // CAP
    per_tile = LANES // CAP
    count = arrived_ref.shape[0] // 8 // per_tile
    halves = []
    for half in range(2):
        pieces = []
        for tile in range(count):
            joined = None
            for m in range(per_tile):
                at = (tile * per_tile + m) * 8
                block = arrived_ref[at : at + 8, :]
                place = (m + 2 * half) % per_tile
                joined = block if joined is None else jnp.where(lane == place, block, joined)
            pieces.append(joined)
        index = jnp.maximum(inverse_row, 0)
        if half:
            index = jnp.bitwise_or(
                jnp.bitwise_and(index, -LANES), jnp.bitwise_and(index + LANES // 2, LANES - 1)
            )
        picked = [
            pick(pieces, jnp.broadcast_to(part, (8, LANES))) for part in tiles_of(index)
        ]
        halves.append(jnp.concatenate(picked, axis=1))
    rows = jnp.concatenate(halves, axis=0)
    return jnp.where(inverse_row >= 0, rows, 0.0)


def restrict(basis_ref, residual, part_ref):
    residual = residual[:TRACE]
    for v in range(CVEC):
        product = basis_ref[v] * residual
        folded = product[:, :LANES] + product[:, LANES : 2 * LANES] + product[:, 2 * LANES :]
        part_ref[v : v + 1, :] = jnp.sum(folded, axis=0, keepdims=True)
    return jnp.sum(part_ref[...], axis=1, keepdims=True)


def start_coarse(blocks_ref, basis_ref, residual, part_ref, send_ref):
    column = restrict(basis_ref, residual, part_ref)
    start = matvec(blocks_ref[:CVEC, :], as_row(column, column)[:, :CVEC])
    send_ref[...] = jnp.broadcast_to(as_row(start, start), send_ref.shape)


def first_kernel(
    count_ref, pairs_ref, slots_ref, load_ref, link_ref, blocks_ref, couple_hbm, basis_hbm,
    trace_ref, inverse_ref, send_ref,
    couple_ref, basis_ref, sum_ref, part_ref, sems,
):
    couple_copy = pltpu.make_async_copy(couple_hbm, couple_ref, sems.at[0])
    basis_copy = pltpu.make_async_copy(basis_hbm, basis_ref, sems.at[1])
    couple_copy.start()
    basis_copy.start()
    live = live_row(count_ref[0, 0])
    slot = lax.broadcasted_iota(jnp.int32, (CAP, FB), 0)
    face = lax.broadcasted_iota(jnp.int32, (CAP, FB), 1)
    found = jnp.zeros((CAP, FB), jnp.int32)
    for j in range(slots_ref.shape[1]):
        named = (slots_ref[:, j : j + 1] == face) & (slot < pairs_ref[0, j])
        found = found + jnp.where(named, slot + (j * CAP + 1), 0)
    inverse = jnp.sum(found, axis=0, keepdims=True) - 1
    inverse_ref[...] = inverse
    interface = (inverse >= 0).astype(f32)
    sum_ref[...] = jnp.zeros_like(sum_ref)
    trace_ref[...] = jnp.zeros_like(trace_ref)
    source = live * load_ref[...]
    trace_ref[:TRACE, :] = source
    source = trace_ref[...]
    trace = omega_step * source
    couple_copy.wait()
    for sweep in range(1, SWEEPS):
        trace = trace + omega_step * (
            source - couple_apply(couple_ref, link_ref, trace, live, interface, sum_ref)
        )
    trace_ref[...] = trace
    residual = source - couple_apply(couple_ref, link_ref, trace, live, interface, sum_ref)
    basis_copy.wait()
    start_coarse(blocks_ref, basis_ref, residual, part_ref, send_ref)


def local_kernel(
    count_ref, arrived_ref, inverse_ref, load_ref, link_ref, blocks_ref, old_ref, couple_hbm, basis_hbm,
    trace_ref, robin_ref, send_ref,
    couple_ref, basis_ref, sum_ref, part_ref, sems,
):
    couple_copy = pltpu.make_async_copy(couple_hbm, couple_ref, sems.at[0])
    basis_copy = pltpu.make_async_copy(basis_hbm, basis_ref, sems.at[1])
    couple_copy.start()
    basis_copy.start()
    live = live_row(count_ref[0, 0])
    inverse = inverse_ref[...]
    interface = (inverse >= 0).astype(f32)
    sum_ref[...] = jnp.zeros_like(sum_ref)
    robin = unpack_slots(arrived_ref, inverse)
    robin_ref[...] = robin
    trace_ref[...] = jnp.zeros_like(trace_ref)
    trace_ref[:TRACE, :] = load_ref[...]
    source = live * (trace_ref[...] + robin)
    trace = old_ref[...]
    couple_copy.wait()
    for sweep in range(SWEEPS):
        trace = trace + omega_step * (
            source - couple_apply(couple_ref, link_ref, trace, live, interface, sum_ref)
        )
    trace_ref[...] = trace
    residual = source - couple_apply(couple_ref, link_ref, trace, live, interface, sum_ref)
    basis_copy.wait()
    start_coarse(blocks_ref, basis_ref, residual, part_ref, send_ref)


def jacobi(blocks_ref, start_row, neighbour_rows):
    total = None
    for k in range(KC):
        term = blocks_ref[pl.ds((k + 1) * CVEC, CVEC), :] * neighbour_rows[k]
        total = term if total is None else total + term
    coupled = jnp.sum(total, axis=1, keepdims=True)
    step = matvec(blocks_ref[:CVEC, :], as_row(coupled, coupled)[:, :CVEC])
    start = jnp.sum(jnp.where(eye(0)[:, :CVEC], start_row, 0.0), axis=1, keepdims=True)
    return start - step


def sweep_kernel(place_ref, own_ref, partner_ref, blocks_ref, twin_ref, send_ref, stack_ref):
    rows = own_ref.shape[0]
    stack_ref[:rows, :] = own_ref[...]
    stack_ref[rows:, :] = partner_ref[...]

    def row(which, k):
        return stack_ref[pl.ds(place_ref[which, k], 1), :][:, :CVEC]

    columns = [
        jacobi(matrices, row(which, KC), [row(which, k) for k in range(KC)])
        for which, matrices in ((0, blocks_ref), (1, twin_ref))
    ]
    send_ref[...] = jnp.broadcast_to(as_row(*columns), send_ref.shape)


def correct_kernel(
    first, last, place_ref, meta_ref, start_ref, swept_ref, blocks_ref, slots_ref, trace_ref, *rest
):
    if first:
        basis_hbm, *rest = rest
    else:
        robin_ref, basis_hbm, *rest = rest
    if last:
        out_ref, coef_ref, packed_ref, basis_ref, spread_ref, sems = rest
    else:
        out_ref, packed_ref, basis_ref, spread_ref, sems = rest
    basis_copy = pltpu.make_async_copy(basis_hbm, basis_ref, sems.at[0])
    basis_copy.start()

    def row(k):
        whole = swept_ref[pl.ds(place_ref[2, k], 1), :]
        moved = pltpu.roll(whole, CVEC, 1)
        return jnp.where(place_ref[3, k] > 0, moved, whole)[:, :CVEC]

    column = jacobi(blocks_ref, start_ref[:1, :CVEC], [row(k) for k in range(KC)])
    if last:
        coef_ref[...] = as_row(column, column)[:, :CVEC]
    spread_ref[...] = jnp.broadcast_to(column, spread_ref.shape)
    live = live_row(meta_ref[0, 0])
    basis_copy.wait()
    parts = [None] * 4
    for v in range(CVEC):
        scale = spread_ref[v : v + 1, :]
        term = basis_ref[v] * jnp.concatenate([scale] * (FB // LANES), axis=1)
        parts[v % 4] = term if parts[v % 4] is None else parts[v % 4] + term
    correction = live * ((parts[0] + parts[1]) + (parts[2] + parts[3]))
    grown = trace_ref[...]
    trace = grown[:TRACE] + correction
    if last:
        out_ref[...] = trace
    if first:
        outgoing = 2.0 * robin_weight * trace
    else:
        outgoing = 2.0 * robin_weight * trace - robin_ref[:TRACE, :]
    packed_ref[0:ROWS, :] = jnp.zeros((ROWS, LANES), f32)
    rows_ref = out_ref if not last else None
    if not last:
        rows_ref[...] = grown
        rows_ref[:TRACE, :] = trace
    pad = jnp.concatenate([outgoing, jnp.zeros((ROWS - TRACE, FB), f32)], axis=0)
    upper = tiles_of(pad[:8])
    lower = tiles_of(pad[8:])
    lane = lax.broadcasted_iota(jnp.int32, (8, LANES), 1) // CAP
    mine = lane == meta_ref[0, 1]
    for j in range(slots_ref.shape[0]):
        index = jnp.broadcast_to(slots_ref[j : j + 1, :], (8, LANES))
        packed_ref[j * 8 : (j + 1) * 8, :] = jnp.where(mine, pick(upper, index), pick(lower, index))


def robin_kernel(arrived_ref, inverse_ref, out_ref):
    out_ref[...] = unpack_slots(arrived_ref, inverse_ref[...])[:TRACE]


SMEM = pl.BlockSpec(memory_space=pltpu.SMEM)
VMEM = pl.BlockSpec(memory_space=pltpu.VMEM)
HBM = pl.BlockSpec(memory_space=pl.ANY)


def call(kernel, name, in_specs, outs, scratch, limit_mib):
    return pl.pallas_call(
        kernel,
        name=name,
        out_shape=[jax.ShapeDtypeStruct(shape, dtype) for shape, dtype in outs],
        in_specs=in_specs,
        out_specs=[VMEM] * len(outs),
        scratch_shapes=scratch,
        compiler_params=pltpu.CompilerParams(vmem_limit_bytes=limit_mib << 20),
    )


COUPLE = pltpu.VMEM((LINKS + 1, TRACE, TRACE, FB), jnp.bfloat16)
BASIS = pltpu.VMEM((CVEC, TRACE, FB), f32)


def pair_groups(groups, peers):
    return [[(2 * m + h) * peers + s for h in range(2) for s in range(peers)] for m in range(groups // 2)]


def partner_pairs(groups):
    pairs = []
    for m in range(groups // 2):
        odd, even = 2 * m + 1, (2 * m + 2) % groups
        pairs += [(odd, even), (even, odd)]
    return pairs


def body(
    load, couple, face_link, face_count, slot_face, pair_count, basis, coarse_inverse, coarse_block, coarse_link
):
    groups, peers = lax.axis_size("grp"), lax.axis_size("sub")
    group, own = lax.axis_index("grp"), lax.axis_index("sub")
    blocks = pair_groups(groups, peers)
    partners = partner_pairs(groups)
    rows = 2 * peers

    def exchange(send):
        arrived = lax.all_to_all(
            send.reshape(rows, 1, LANES), ("grp", "sub"), 0, 0, axis_index_groups=blocks, tiled=True
        )
        return arrived.reshape(rows, LANES)

    links = coarse_link[0, 0]
    tail = jnp.zeros((8, CVEC), f32).at[0, :KC].set(links.astype(f32))
    packed = jnp.concatenate(
        [coarse_inverse[0, 0], coarse_block[0, 0].reshape(KC * CVEC, CVEC), tail], axis=0
    )
    twin = lax.ppermute(packed, "grp", partners)
    twin_links = twin[(KC + 1) * CVEC, :KC].astype(jnp.int32)

    base = group // 2 * 2
    odd = group - base
    partner = jnp.where(odd == 1, (group + 1) % groups, (group + groups - 1) % groups)
    partner_base = partner // 2 * 2
    ids = jnp.stack(
        [
            jnp.concatenate([links, (group * peers + own)[None]]),
            jnp.concatenate([twin_links, (partner * peers + own)[None]]),
        ]
    )
    in_pair = ids // peers // 2 * 2 == base
    first_places = jnp.where(in_pair, ids - base * peers, rows + ids - partner_base * peers)
    first_places = jnp.clip(first_places, 0, 2 * rows - 1)
    ahead = ids[0] // peers - base
    across = (ahead < 0) | (ahead > 1)
    second_places = jnp.where(ahead > 0, peers, 0) + ids[0] % peers
    places = jnp.concatenate([first_places, second_places[None], across.astype(jnp.int32)[None]], axis=0)

    count = face_count.astype(jnp.int32)
    meta = jnp.stack([face_count[0, 0], own % (LANES // CAP)])[None]
    own_slots = slot_face[0, 0]
    wide_slots = jnp.tile(own_slots, (1, LANES // CAP))
    face_links = face_link[0, 0]
    load_rows, couple_rows, basis_rows = load[0, 0], couple[0, 0], basis[0, 0]

    field = ((ROWS, FB), f32)
    sends = ((rows, LANES), f32)
    work = [
        COUPLE,
        BASIS,
        pltpu.VMEM((ROWS, FB), f32),
        pltpu.VMEM((CVEC, LANES), f32),
        pltpu.SemaphoreType.DMA((2,)),
    ]
    arrived = robin = inverse = trace = None
    for outer_step in range(ITERS):
        first, last = outer_step == 0, outer_step == ITERS - 1
        if first:
            trace, inverse, start = call(
                first_kernel,
                "first",
                [SMEM, SMEM, VMEM, VMEM, VMEM, VMEM, HBM, HBM],
                [field, ((1, FB), jnp.int32), sends],
                work,
                16,
            )(
                count, pair_count[0], own_slots.T, load_rows, face_links, packed, couple_rows, basis_rows
            )
        else:
            trace, robin, start = call(
                local_kernel,
                "local",
                [SMEM, VMEM, VMEM, VMEM, VMEM, VMEM, VMEM, HBM, HBM],
                [field, field, sends],
                work,
                16,
            )(
                count, arrived, inverse, load_rows, face_links, packed, trace, couple_rows, basis_rows
            )
        window = exchange(start)
        beyond = lax.ppermute(window, "grp", partners)
        (swept,) = call(
            sweep_kernel,
            "sweep",
            [SMEM, VMEM, VMEM, VMEM, VMEM],
            [sends],
            [pltpu.VMEM((2 * rows, LANES), f32)],
            8,
        )(places, window, beyond, packed, twin)
        swept = exchange(swept)
        outs = [((TRACE, FB), f32), ((1, CVEC), f32)] if last else [field]
        outs = outs + [((peers * 8, LANES), f32)]
        operands = [places, meta, start, swept, packed, wide_slots, trace]
        operands += ([] if first else [robin]) + [basis_rows]
        results = call(
            functools.partial(correct_kernel, first, last),
            "correct",
            [SMEM, SMEM] + [VMEM] * (len(operands) - 3) + [HBM],
            outs,
            [BASIS, pltpu.VMEM((CVEC, LANES), f32), pltpu.SemaphoreType.DMA((1,))],
            16,
        )(*operands)
        trace, outgoing = results[0], results[-1]
        if last:
            coefficients = results[1]
        arrived = lax.all_to_all(outgoing.reshape(peers, 8, LANES), "sub", 0, 0, tiled=True)
        arrived = arrived.reshape(peers * 8, LANES)
    (robin,) = call(robin_kernel, "robin", [VMEM, VMEM], [((TRACE, FB), f32)], [], 8)(arrived, inverse)
    return (trace[None, None], robin[None, None], coefficients[None])


def solution(mesh):
    in_specs = (
        P("grp", "sub", None, None),
        P("grp", "sub", None, None, None, None),
        P("grp", "sub", None, None),
        P("grp", "sub"),
        P("grp", "sub", None, None),
        P("grp", "sub", None),
        P("grp", "sub", None, None, None),
        P("grp", "sub", None, None),
        P("grp", "sub", None, None, None),
        P("grp", "sub", None),
    )
    out_specs = (P("grp", "sub", None, None), P("grp", "sub", None, None), P("grp", "sub", None))
    return jax.shard_map(body, mesh=mesh, in_specs=in_specs, out_specs=out_specs, check_vma=False)
```

time: 353 us -> 173 us (0.49)
  the two profiles are of different devices: /device:TPU:513 before, /device:TPU:1 now
where the time goes in v1:
time: 173 us
  blocking collectives  68.7 us (40%)
  starting transfers between devices  40.8 us (24%)
  waiting for transfers between devices  40 us (23%)
  Pallas kernels  13.9 us (8%)
  local copies, waits for them, and re-layouts  5.76 us (3%)
  other arithmetic  1.98 us (1%)
    all_to_all x4, blocking collectives, exchange(): lax.all_to_all(send.reshape(rows, 1, LANES), ('grp', 'sub'), 0, 0, axis_i...  46.6 us
    all_to_all x2, blocking collectives, body(): lax.all_to_all(outgoing.reshape(peers, 8, LANES), 'sub', 0, 0, tiled=True)  22 us
    ppermute x3, waiting for transfers between devices, body(): beyond = lax.ppermute(window, 'grp', partners)  17.5 us
    ppermute x1, starting transfers between devices, body(): twin = lax.ppermute(packed, 'grp', partners)  17.3 us
    all_to_all x2, waiting for transfers between devices, exchange(): lax.all_to_all(send.reshape(rows, 1, LANES), ('grp', 'sub'), 0, 0, axis_i...  15.3 us
    all_to_all x2, starting transfers between devices, exchange(): lax.all_to_all(send.reshape(rows, 1, LANES), ('grp', 'sub'), 0, 0, axis_i...  13.7 us
    all_to_all x1, waiting for transfers between devices, body(): lax.all_to_all(outgoing.reshape(peers, 8, LANES), 'sub', 0, 0, tiled=True)  7.19 us
    ppermute x3, starting transfers between devices, body(): beyond = lax.ppermute(window, 'grp', partners)  5.73 us
  transfers between devices with their start and end apart: 7, of which 6 were waited for; matrix products, arithmetic and copies ran while one was open for 3% of the time, Pallas kernels for 2%

profile of v1, /device:TPU:1, one launch (start us, length us, event | category | flops | bytes accessed | tf_op | source)
XLA Modules:
  0.0 172.6 jit_solution(6960305672131793117)
XLA Ops:
  0.6 0.7 bitcast_convert_fusion
  1.3 0.9 select_maximum_fusion.blocks_ref
  2.2 17.3 %collective-permute-start = (f32[456,64]{1,0:T(8,128)S(1)}, f32[456,64]{1,0:T(8,128)S(1)}, u32[]{:S(2)}, u32[]{:S(2)}) collective-permute-start(f32[456,64]{1,0:T(8,128)S(1)} %select_maximum_fusion.blocks_ref), channel_id=1, source_target_pairs={{16,32},{32,16},{48,64},{64,48},{80,96},{96,80},{112,128},{128,112... | collective-permute-start | bytes 350216 | tf_op jit(solution)/shard_map/ppermute | solution.py:324
  20.2 0.7 copy.41
  20.9 0.8 copy.19
  21.7 0.9 copy.40
  22.5 1.2 copy.39
  23.7 0.0 copy-start
  23.8 0.9 copy.38
  24.6 0.0 copy-start.3
  24.6 0.0 copy-done
  24.7 0.0 copy-start.2
  24.7 2.7 %first.1 = (f32[16,384]{1,0:T(8,128)S(1)}, s32[1,384]{1,0:T(1,128)S(1)}, f32[32,128]{1,0:T(8,128)}) custom-call(s32[1,1]{1,0:T(1,128)} %copy.42.count_ref, s32[1,16]{1,0:T(1,128)S(1)} %bitcast.105, s32[32,16]{1,0:T(8,128)S(1)} %bitcast.93, f32[15,384]{1,0:T(8,128)S(1)} %bitcast.78, s32[3,384]{1,0:T(4,128)S(1)} %bitcast.85, ...), custom_call_target="tpu_custom_call" | custom-call | tf_op jit(solution)/shard_map/first/pallas_call | solution.py:365
  27.4 8.2 %all-to-all-start = ((f32[32,1,128]{2,1,0:T(1,128)}), f32[32,1,128]{2,1,0:T(1,128)S(1)}, u32[]{:S(2)}, u32[]{:S(2)}) async-start(f32[32,1,128]{2,1,0:T(1,128)} %bitcast.19), calls=%async_computation | async-start | bytes 32768 | tf_op jit(solution)/shard_map/all_to_all | solution.py:314
  35.6 0.1 fusion.1
  35.7 0.1 add_bitcast_fusion
  35.8 7.6 %all-to-all-done = f32[32,1,128]{2,1,0:T(1,128)S(1)} async-done(((f32[32,1,128]{2,1,0:T(1,128)}), f32[32,1,128]{2,1,0:T(1,128)S(1)}, u32[]{:S(2)}, u32[]{:S(2)}) %all-to-all-start) | async-done | bytes 16416 | tf_op jit(solution)/shard_map/all_to_all | solution.py:314
  43.4 1.9 %collective-permute-start.1 = (f32[32,128]{1,0:T(8,128)S(1)}, f32[32,128]{1,0:T(8,128)S(1)}, u32[]{:S(2)}, u32[]{:S(2)}) collective-permute-start(f32[32,128]{1,0:T(8,128)S(1)} %bitcast.94), channel_id=1, source_target_pairs={{16,32},{32,16},{48,64},{64,48},{80,96},{96,80},{112,128},{128,112... | collective-permute-start | bytes 49160 | tf_op jit(solution)/shard_map/ppermute | solution.py:387
  45.3 0.0 collective-permute-done.twin_ref
  45.3 0.1 add_bitcast_fusion.1
  45.4 5.7 %collective-permute-done.1.partner_ref = f32[32,128]{1,0:T(8,128)S(1)} collective-permute-done((f32[32,128]{1,0:T(8,128)S(1)}, f32[32,128]{1,0:T(8,128)S(1)}, u32[]{:S(2)}, u32[]{:S(2)}) %collective-permute-start.1) | collective-permute-done | bytes 16416 | tf_op jit(solution)/shard_map/ppermute | solution.py:387
  51.2 1.4 sweep.3
  52.6 5.4 %all-to-all-start.1 = ((f32[32,1,128]{2,1,0:T(1,128)}), f32[32,1,128]{2,1,0:T(1,128)S(1)}, u32[]{:S(2)}, u32[]{:S(2)}) async-start(f32[32,1,128]{2,1,0:T(1,128)} %bitcast.22), calls=%async_computation.1 | async-start | bytes 32768 | tf_op jit(solution)/shard_map/all_to_all | solution.py:314
  58.0 0.1 add_bitcast_fusion.2.meta_ref
  58.1 0.1 tile.9.slots_ref
  58.2 7.7 %all-to-all-done.1 = f32[32,1,128]{2,1,0:T(1,128)S(1)} async-done(((f32[32,1,128]{2,1,0:T(1,128)}), f32[32,1,128]{2,1,0:T(1,128)S(1)}, u32[]{:S(2)}, u32[]{:S(2)}) %all-to-all-start.1) | async-done | bytes 16416 | tf_op jit(solution)/shard_map/all_to_all | solution.py:314
  65.9 1.5 correct.3
  67.4 11.0 %all_to_all.45 = f32[16,8,128]{2,1,0:T(8,128)S(1)} all-to-all(f32[16,8,128]{2,1,0:T(8,128)S(1)} %bitcast.103), channel_id=1, replica_groups=mesh['grp'=48,'sub'=16] {'sub'}, dimensions={0} | all-to-all | bytes 131072 | tf_op jit(solution)/shard_map/all_to_all | solution.py:412
  78.4 1.7 local.2
  80.1 10.8 %all_to_all.46 = f32[32,1,128]{2,1,0:T(1,128)S(1)} all-to-all(f32[32,1,128]{2,1,0:T(1,128)S(1)} %bitcast.89), channel_id=1, replica_groups={{0,1,2,3,4,5,6,7,8,9,10,11,12,13,14,15,16,17,18,19,20,21,22,23,24,25,26..., dimensions={0} | all-to-all | bytes 32768 | tf_op jit(solution)/shard_map/all_to_all | solution.py:314
  90.9 1.9 %collective-permute-start.2 = (f32[32,128]{1,0:T(8,128)S(1)}, f32[32,128]{1,0:T(8,128)S(1)}, u32[]{:S(2)}, u32[]{:S(2)}) collective-permute-start(f32[32,128]{1,0:T(8,128)S(1)} %bitcast.98), channel_id=1, source_target_pairs={{16,32},{32,16},{48,64},{64,48},{80,96},{96,80},{112,128},{128,112... | collective-permute-start | bytes 49160 | tf_op jit(solution)/shard_map/ppermute | solution.py:387
  92.8 5.9 %collective-permute-done.2.partner_ref = f32[32,128]{1,0:T(8,128)S(1)} collective-permute-done((f32[32,128]{1,0:T(8,128)S(1)}, f32[32,128]{1,0:T(8,128)S(1)}, u32[]{:S(2)}, u32[]{:S(2)}) %collective-permute-start.2) | collective-permute-done | bytes 16416 | tf_op jit(solution)/shard_map/ppermute | solution.py:387
  98.7 0.8 sweep.4
  99.5 12.5 %all_to_all.47 = f32[32,1,128]{2,1,0:T(1,128)S(1)} all-to-all(f32[32,1,128]{2,1,0:T(1,128)S(1)} %bitcast.101), channel_id=1, replica_groups={{0,1,2,3,4,5,6,7,8,9,10,11,12,13,14,15,16,17,18,19,20,21,22,23,24,25,26..., dimensions={0} | all-to-all | bytes 32768 | tf_op jit(solution)/shard_map/all_to_all | solution.py:314
  112.1 1.3 correct.4
  113.4 11.0 %all_to_all.48 = f32[16,8,128]{2,1,0:T(8,128)S(1)} all-to-all(f32[16,8,128]{2,1,0:T(8,128)S(1)} %bitcast.102), channel_id=1, replica_groups=mesh['grp'=48,'sub'=16] {'sub'}, dimensions={0} | all-to-all | bytes 131072 | tf_op jit(solution)/shard_map/all_to_all | solution.py:412
  124.4 1.7 local.3
  126.1 10.8 %all_to_all.49 = f32[32,1,128]{2,1,0:T(1,128)S(1)} all-to-all(f32[32,1,128]{2,1,0:T(1,128)S(1)} %bitcast.88), channel_id=1, replica_groups={{0,1,2,3,4,5,6,7,8,9,10,11,12,13,14,15,16,17,18,19,20,21,22,23,24,25,26..., dimensions={0} | all-to-all | bytes 32768 | tf_op jit(solution)/shard_map/all_to_all | solution.py:314
  136.9 1.9 %collective-permute-start.3 = (f32[32,128]{1,0:T(8,128)S(1)}, f32[32,128]{1,0:T(8,128)S(1)}, u32[]{:S(2)}, u32[]{:S(2)}) collective-permute-start(f32[32,128]{1,0:T(8,128)S(1)} %bitcast.96), channel_id=1, source_target_pairs={{16,32},{32,16},{48,64},{64,48},{80,96},{96,80},{112,128},{128,112... | collective-permute-start | bytes 49160 | tf_op jit(solution)/shard_map/ppermute | solution.py:387
  138.8 5.9 %collective-permute-done.3.partner_ref = f32[32,128]{1,0:T(8,128)S(1)} collective-permute-done((f32[32,128]{1,0:T(8,128)S(1)}, f32[32,128]{1,0:T(8,128)S(1)}, u32[]{:S(2)}, u32[]{:S(2)}) %collective-permute-start.3) | collective-permute-done | bytes 16416 | tf_op jit(solution)/shard_map/ppermute | solution.py:387
  144.7 0.8 sweep.5
  145.5 12.5 %all_to_all.50 = f32[32,1,128]{2,1,0:T(1,128)S(1)} all-to-all(f32[32,1,128]{2,1,0:T(1,128)S(1)} %bitcast.100), channel_id=1, replica_groups={{0,1,2,3,4,5,6,7,8,9,10,11,12,13,14,15,16,17,18,19,20,21,22,23,24,25,26..., dimensions={0} | all-to-all | bytes 32768 | tf_op jit(solution)/shard_map/all_to_all | solution.py:314
  158.0 1.9 %correct.5 = (f32[15,384]{1,0:T(8,128)S(1)}, f32[1,64]{1,0:T(1,128)}, f32[128,128]{1,0:T(8,128)}) custom-call(s32[4,7]{1,0:T(4,128)S(1)} %pad_add_fusion.place_ref, s32[1,2]{1,0:T(1,128)S(1)} %add_bitcast_fusion.2.meta_ref, f32[32,128]{1,0:T(8,128)S(1)} %get-tuple-element.41.start_ref, f32[32,128]{1,0:T(8,128)S(1)} %bitcast.91, ...), custom_call_target="tpu_custom_call" | custom-call | tf_op jit(solution)/shard_map/correct/pallas_call | solution.py:401
  160.0 4.1 %all-to-all-start.8 = ((f32[16,8,128]{2,1,0:T(8,128)}), f32[16,8,128]{2,1,0:T(8,128)S(1)}, u32[]{:S(2)}, u32[]{:S(2)}) async-start(f32[16,8,128]{2,1,0:T(8,128)} %bitcast.42), calls=%async_computation.8 | async-start | bytes 131072 | tf_op jit(solution)/shard_map/all_to_all | solution.py:412
  164.0 0.6 copy.29
  164.7 7.2 %all-to-all-done.8 = f32[16,8,128]{2,1,0:T(8,128)S(1)} async-done(((f32[16,8,128]{2,1,0:T(8,128)}), f32[16,8,128]{2,1,0:T(8,128)S(1)}, u32[]{:S(2)}, u32[]{:S(2)}) %all-to-all-start.8) | async-done | bytes 65568 | tf_op jit(solution)/shard_map/all_to_all | solution.py:412
  171.9 0.1 robin.1
  172.0 0.6 copy.30
  (9 shorter events, 0.1 us)
Async XLA Ops:
  2.2 43.0 %collective-permute-start = (f32[456,64]{1,0:T(8,128)S(1)}, f32[456,64]{1,0:T(8,128)S(1)}, u32[]{:S(2)}, u32[]{:S(2)}) collective-permute-start(f32[456,64]{1,0:T(8,128)S(1)} %select_maximum_fusion.blocks_ref), channel_id=1, source_target_pairs={{16,32},{32,16},{48,64},{64,48},{80,96},{96,80},{112,128},{128,112... | collective-permute-start | bytes 350216 | tf_op jit(solution)/shard_map/ppermute | solution.py:324
  21.7 2.1 %copy-start.1 = (f32[1,1,64,15,384]{4,2,3,1,0:T(8,128)S(1)}, f32[1,1,64,15,384]{4,2,3,1,0:T(8,128)}, u32[]{:S(2)}) copy-start(f32[1,1,64,15,384]{4,2,3,1,0:T(8,128)} %param.18) | copy-start | bytes 4423684
  23.7 0.9 copy-start
  24.6 11.0 %copy-start.3 = (s32[1,1,6]{2,1,0:T(1,128)S(1)}, s32[1,1,6]{2,1,0:T(1,128)}, u32[]{:S(2)}) copy-start(s32[1,1,6]{2,1,0:T(1,128)} %param.21) | copy-start | bytes 76
  24.7 33.4 %copy-start.2 = (s32[1,1,16,32]{3,2,1,0:T(8,128)S(1)}, s32[1,1,16,32]{3,2,1,0:T(8,128)}, u32[]{:S(2)}) copy-start(s32[1,1,16,32]{3,2,1,0:T(8,128)} %param.16) | copy-start | bytes 6148
  27.4 16.0 %all-to-all-start = ((f32[32,1,128]{2,1,0:T(1,128)}), f32[32,1,128]{2,1,0:T(1,128)S(1)}, u32[]{:S(2)}, u32[]{:S(2)}) async-start(f32[32,1,128]{2,1,0:T(1,128)} %bitcast.19), calls=%async_computation | async-start | bytes 32768 | tf_op jit(solution)/shard_map/all_to_all | solution.py:314
  43.4 7.8 %collective-permute-start.1 = (f32[32,128]{1,0:T(8,128)S(1)}, f32[32,128]{1,0:T(8,128)S(1)}, u32[]{:S(2)}, u32[]{:S(2)}) collective-permute-start(f32[32,128]{1,0:T(8,128)S(1)} %bitcast.94), channel_id=1, source_target_pairs={{16,32},{32,16},{48,64},{64,48},{80,96},{96,80},{112,128},{128,112... | collective-permute-start | bytes 49160 | tf_op jit(solution)/shard_map/ppermute | solution.py:387
  52.6 13.4 %all-to-all-start.1 = ((f32[32,1,128]{2,1,0:T(1,128)}), f32[32,1,128]{2,1,0:T(1,128)S(1)}, u32[]{:S(2)}, u32[]{:S(2)}) async-start(f32[32,1,128]{2,1,0:T(1,128)} %bitcast.22), calls=%async_computation.1 | async-start | bytes 32768 | tf_op jit(solution)/shard_map/all_to_all | solution.py:314
  90.9 7.8 %collective-permute-start.2 = (f32[32,128]{1,0:T(8,128)S(1)}, f32[32,128]{1,0:T(8,128)S(1)}, u32[]{:S(2)}, u32[]{:S(2)}) collective-permute-start(f32[32,128]{1,0:T(8,128)S(1)} %bitcast.98), channel_id=1, source_target_pairs={{16,32},{32,16},{48,64},{64,48},{80,96},{96,80},{112,128},{128,112... | collective-permute-start | bytes 49160 | tf_op jit(solution)/shard_map/ppermute | solution.py:387
  136.9 7.8 %collective-permute-start.3 = (f32[32,128]{1,0:T(8,128)S(1)}, f32[32,128]{1,0:T(8,128)S(1)}, u32[]{:S(2)}, u32[]{:S(2)}) collective-permute-start(f32[32,128]{1,0:T(8,128)S(1)} %bitcast.96), channel_id=1, source_target_pairs={{16,32},{32,16},{48,64},{64,48},{80,96},{96,80},{112,128},{128,112... | collective-permute-start | bytes 49160 | tf_op jit(solution)/shard_map/ppermute | solution.py:387
  160.0 11.9 %all-to-all-start.8 = ((f32[16,8,128]{2,1,0:T(8,128)}), f32[16,8,128]{2,1,0:T(8,128)S(1)}, u32[]{:S(2)}, u32[]{:S(2)}) async-start(f32[16,8,128]{2,1,0:T(8,128)} %bitcast.42), calls=%async_computation.8 | async-start | bytes 131072 | tf_op jit(solution)/shard_map/all_to_all | solution.py:412

commit v2 on v1

v2 whole, which is shorter than its diff:
```python
import functools

import jax
import jax.numpy as jnp
from jax import lax
from jax.experimental import pallas as pl
from jax.experimental.pallas import tpu as pltpu
from jax.sharding import PartitionSpec as P

TRACE = 15
ROWS = 16
FB = 384
CAP = 32
LANES = 128
LINKS = 3
CVEC = 64
KC = 6
ITERS = 3
SWEEPS = 2

robin_weight = 1.0
omega_step = 0.2
f32 = jnp.float32


def pick(pieces, index):
    low = jnp.bitwise_and(index, LANES - 1)
    high = jnp.right_shift(index, 7)
    out = None
    for at, piece in enumerate(pieces):
        taken = jnp.take_along_axis(piece, low, axis=1, mode="promise_in_bounds")
        out = taken if out is None else jnp.where(high == at, taken, out)
    return out


def tiles_of(rows):
    return [rows[:, t * LANES : (t + 1) * LANES] for t in range(rows.shape[1] // LANES)]


def pick_faces(rows, index_row):
    pieces = tiles_of(rows)
    picked = [
        pick(pieces, jnp.broadcast_to(part, (rows.shape[0], LANES))) for part in tiles_of(index_row)
    ]
    return jnp.concatenate(picked, axis=1)


def pick_rows(blocks, index):
    low = jnp.bitwise_and(index, 7)
    high = jnp.right_shift(index, 3)
    out = None
    for at, block in enumerate(blocks):
        taken = jnp.take_along_axis(block, low, axis=0, mode="promise_in_bounds")
        out = taken if out is None else jnp.where(high == at, taken, out)
    return out


def blocks_of(ref, rows):
    return [ref[at : at + 8, :] for at in range(0, rows, 8)]


def eye(offset):
    row = lax.broadcasted_iota(jnp.int32, (CVEC, LANES), 0)
    lane = lax.broadcasted_iota(jnp.int32, (CVEC, LANES), 1)
    return lane == row + offset


def as_row(low, high=None):
    spread = jnp.where(eye(0), low, 0.0)
    if high is not None:
        spread = spread + jnp.where(eye(CVEC), high, 0.0)
    return jnp.sum(spread, axis=0, keepdims=True)


def low_lanes():
    return lax.broadcasted_iota(jnp.int32, (1, LANES), 1) < CVEC


def couple_apply(couple_ref, link_ref, trace, live, interface, stack_ref):
    stack_ref[0] = trace
    for k in range(LINKS):
        stack_ref[k + 1] = pick_faces(trace, link_ref[k])
    sums = []
    for k in range(LINKS + 1):
        total = None
        for b in range(TRACE):
            term = couple_ref[k, b].astype(f32) * stack_ref[k, b : b + 1, :]
            total = term if total is None else total + term
        sums.append(total)
    total = (sums[0] + sums[1]) + (sums[2] + sums[3])
    return live * (total + robin_weight * interface * trace[:TRACE])


def unpack_slots(arrived_ref, inverse_row):
    lane = lax.broadcasted_iota(jnp.int32, (8, LANES), 1) // CAP
    per_tile = LANES // CAP
    count = arrived_ref.shape[0] // 8 // per_tile
    halves = []
    for half in range(2):
        pieces = []
        for tile in range(count):
            joined = None
            for m in range(per_tile):
                at = (tile * per_tile + m) * 8
                block = arrived_ref[at : at + 8, :]
                place = (m + 2 * half) % per_tile
                joined = block if joined is None else jnp.where(lane == place, block, joined)
            pieces.append(joined)
        index = jnp.maximum(inverse_row, 0)
        if half:
            index = jnp.bitwise_or(
                jnp.bitwise_and(index, -LANES), jnp.bitwise_and(index + LANES // 2, LANES - 1)
            )
        picked = [
            pick(pieces, jnp.broadcast_to(part, (8, LANES))) for part in tiles_of(index)
        ]
        halves.append(jnp.concatenate(picked, axis=1))
    rows = jnp.concatenate(halves, axis=0)
    return jnp.where(inverse_row >= 0, rows, 0.0)


def start_coarse(blocks_ref, basis_ref, residual, rows_ref, send_ref):
    rows_ref[:TRACE, :] = residual
    totals = [None] * (FB // LANES)
    for a in range(TRACE):
        for t in range(len(totals)):
            lanes = slice(t * LANES, (t + 1) * LANES)
            term = basis_ref[a, :, lanes] * rows_ref[a : a + 1, lanes]
            totals[t] = term if totals[t] is None else totals[t] + term
    restricted = jnp.sum(totals[0] + totals[1] + totals[2], axis=1, keepdims=True)
    start = jnp.sum(blocks_ref[:CVEC, :] * as_row(restricted), axis=1, keepdims=True)
    send_ref[...] = jnp.broadcast_to(as_row(start, start), send_ref.shape)


def sweeps(couple_ref, link_ref, source, trace, live, interface, stack_ref, rows_ref, count):
    rows_ref[...] = trace
    trace = trace[:TRACE]
    for sweep in range(count + 1):
        residual = source - couple_apply(
            couple_ref, link_ref, rows_ref[...], live, interface, stack_ref
        )
        if sweep < count:
            trace = trace + omega_step * residual
            rows_ref[:TRACE, :] = trace
    return trace, residual


def place_rows(places):
    row = lax.broadcasted_iota(jnp.int32, (8, LANES), 0)
    low = lax.broadcasted_iota(jnp.int32, (8, LANES), 1) < CVEC
    out = jnp.zeros((8, LANES), jnp.int32)
    for k, (at_low, at_high) in enumerate(places):
        out = jnp.where(row == k, jnp.where(low, at_low, at_high), out)
    return out


def first_kernel(
    groups, peers,
    count_hbm, pairs_hbm, ids_hbm, slots_hbm, load_hbm, link_hbm, matrix_hbm, coupling_hbm, basis_hbm, couple_ref,
    trace_ref, load_out_ref, live_ref, inverse_ref, wide_ref, mine_ref, places_ref, blocks_ref, send_ref,
    stack_ref, rows_ref, count_ref, pairs_ref, ids_ref, slots_ref, load_ref, link_ref, matrix_ref, coupling_ref,
    basis_ref, sems,
):
    moves = [
        pltpu.make_async_copy(source, target, sems.at[at])
        for at, (source, target) in enumerate(
            [
                (count_hbm, count_ref),
                (pairs_hbm, pairs_ref),
                (ids_hbm, ids_ref),
                (slots_hbm, slots_ref),
                (load_hbm, load_ref),
                (link_hbm, link_ref),
                (matrix_hbm, matrix_ref),
                (coupling_hbm, coupling_ref),
                (basis_hbm, basis_ref),
            ]
        )
    ]
    for move in moves:
        move.start()
    group, own = lax.axis_index("grp"), lax.axis_index("sub")
    load_out_ref[...] = jnp.zeros_like(load_out_ref)
    for move in moves[:6]:
        move.wait()

    live = (lax.broadcasted_iota(jnp.int32, (1, FB), 1) < count_ref[0, 0]).astype(f32)
    live_ref[...] = live
    slots = slots_ref[...]
    wide_ref[...] = jnp.concatenate([slots] * (LANES // CAP), axis=1)
    lane = lax.broadcasted_iota(jnp.int32, (8, LANES), 1) // CAP
    mine_ref[...] = (lane == lax.rem(own, LANES // CAP)).astype(jnp.int32)
    columns = slots.T
    slot = lax.broadcasted_iota(jnp.int32, (CAP, FB), 0)
    face = lax.broadcasted_iota(jnp.int32, (CAP, FB), 1)
    found = jnp.zeros((CAP, FB), jnp.int32)
    for j in range(peers):
        named = (columns[:, j : j + 1] == face) & (slot < pairs_ref[0, j])
        found = found + jnp.where(named, slot + (j * CAP + 1), 0)
    inverse = jnp.sum(found, axis=0, keepdims=True) - 1
    inverse_ref[...] = inverse
    interface = (inverse >= 0).astype(f32)

    for a in range(TRACE):
        load_out_ref[a : a + 1, :] = load_ref[a]
    source = live * load_out_ref[...]
    start = omega_step * source
    trace, residual = sweeps(
        couple_ref, link_ref, source[:TRACE], start, live, interface, stack_ref, rows_ref, SWEEPS - 1
    )
    trace_ref[...] = start
    trace_ref[:TRACE, :] = trace

    rows = 2 * peers
    odd = lax.rem(group, 2)
    base = group - odd
    partner = lax.rem(jnp.where(odd == 1, group + 1, group + groups - 1), groups)
    partner_base = partner - lax.rem(partner, 2)

    def place(identity, pair, other):
        inside = (identity >= pair * peers) & (identity < pair * peers + rows)
        return jnp.clip(jnp.where(inside, identity - pair * peers, rows + identity - other * peers), 0, 2 * rows - 1)

    def second(k):
        identity = ids_ref[0, k]
        ahead = lax.div(identity, peers) - base
        across = ((ahead < 0) | (ahead > 1)).astype(jnp.int32)
        return jnp.where(ahead > 0, peers, 0) + lax.rem(identity, peers), across

    myself = group * peers + own
    for at, (pair, other) in enumerate(((base, partner_base), (partner_base, base))):
        spots = [place(ids_ref[0, k], pair, other) for k in range(KC)]
        spots = list(zip(spots[0::2], spots[1::2])) + [(place(myself, pair, other),) * 2]
        index = place_rows(spots)
        if at:
            blocks_ref[(KC // 2 + 1) * CVEC :, :] = index.astype(f32)
        else:
            places_ref[:8, :] = index
    spots = []
    for k in range(0, KC, 2):
        (row_low, across_low), (row_high, across_high) = second(k), second(k + 1)
        spots.append((row_low + rows * across_low, row_high + rows * (1 - across_high)))
    places_ref[8:, :] = place_rows(spots)

    for move in moves[6:]:
        move.wait()
    blocks_ref[:CVEC, :] = jnp.concatenate([matrix_ref[...], jnp.zeros((CVEC, CVEC), f32)], axis=1)
    for k in range(0, KC, 2):
        at = (k // 2 + 1) * CVEC
        blocks_ref[at : at + CVEC, :] = jnp.concatenate([coupling_ref[k], coupling_ref[k + 1]], axis=1)
    start_coarse(blocks_ref, basis_ref, residual, rows_ref, send_ref)


def local_kernel(
    arrived_ref, live_ref, inverse_ref, load_ref, link_ref, blocks_ref, old_ref, couple_ref, basis_ref,
    trace_ref, robin_ref, send_ref,
    stack_ref, rows_ref,
):
    live = live_ref[...]
    inverse = inverse_ref[...]
    interface = (inverse >= 0).astype(f32)
    robin = unpack_slots(arrived_ref, inverse)
    robin_ref[...] = robin
    source = live * (load_ref[...] + robin)
    trace, residual = sweeps(
        couple_ref, link_ref, source[:TRACE], old_ref[...], live, interface, stack_ref, rows_ref, SWEEPS
    )
    trace_ref[...] = robin
    trace_ref[:TRACE, :] = trace
    start_coarse(blocks_ref, basis_ref, residual, rows_ref, send_ref)


def coarse_step(blocks_ref, first, pair_rows):
    total = None
    for k in range(KC // 2):
        matrix = blocks_ref[first + (k + 1) * CVEC : first + (k + 2) * CVEC, :]
        term = matrix * pair_rows[k : k + 1]
        total = term if total is None else total + term
    coupled = jnp.sum(total, axis=1, keepdims=True)
    return jnp.sum(blocks_ref[first : first + CVEC, :] * as_row(coupled), axis=1, keepdims=True)


def sweep_kernel(places_ref, own_ref, partner_ref, blocks_ref, twin_ref, send_ref):
    rows = own_ref.shape[0]
    window = blocks_of(own_ref, rows) + blocks_of(partner_ref, rows)
    own = pick_rows(window, places_ref[:8, :])
    after = rows + (KC // 2 + 1) * CVEC
    twin = pick_rows(window, twin_ref[after : after + 8, :].astype(jnp.int32))
    steps = [coarse_step(blocks_ref, 0, own), coarse_step(twin_ref, rows, twin)]
    at = KC // 2
    swept = jnp.where(low_lanes(), own[at : at + 1], twin[at : at + 1]) - as_row(*steps)
    send_ref[...] = jnp.broadcast_to(swept, send_ref.shape)


def correct_kernel(
    first, last, places_ref, live_ref, mine_ref, start_ref, swept_ref, blocks_ref, slots_ref, trace_ref, *rest
):
    if first:
        basis_ref, *rest = rest
    else:
        robin_ref, basis_ref, *rest = rest
    if last:
        out_ref, coef_ref, packed_ref, rows_ref = rest
    else:
        out_ref, packed_ref, rows_ref = rest
    window = blocks_of(swept_ref, swept_ref.shape[0])
    window = window + [pltpu.roll(block, CVEC, 1) for block in window]
    step = coarse_step(blocks_ref, 0, pick_rows(window, places_ref[8:, :]))
    start = jnp.sum(jnp.where(eye(0), start_ref[:1, :], 0.0), axis=1, keepdims=True)
    column = start - step
    if last:
        coef_ref[...] = as_row(column)[:, :CVEC]
    spread = jnp.broadcast_to(column, (CVEC, LANES))
    live = live_ref[...]
    for a in range(TRACE):
        for t in range(FB // LANES):
            lanes = slice(t * LANES, (t + 1) * LANES)
            rows_ref[a : a + 1, lanes] = jnp.sum(basis_ref[a, :, lanes] * spread, axis=0, keepdims=True)
    rows_ref[TRACE:, :] = jnp.zeros((ROWS - TRACE, FB), f32)
    trace = trace_ref[...] + live * rows_ref[...]
    if last:
        for a in range(TRACE):
            out_ref[a] = trace[a : a + 1]
    else:
        out_ref[...] = trace
    outgoing = 2.0 * robin_weight * trace
    if not first:
        outgoing = outgoing - robin_ref[...]
    upper = tiles_of(outgoing[:8])
    lower = tiles_of(outgoing[8:])
    mine = mine_ref[...] > 0
    for j in range(slots_ref.shape[0]):
        index = jnp.broadcast_to(slots_ref[j : j + 1, :], (8, LANES))
        packed_ref[j * 8 : (j + 1) * 8, :] = jnp.where(mine, pick(upper, index), pick(lower, index))


def robin_kernel(arrived_ref, inverse_ref, out_ref):
    robin = unpack_slots(arrived_ref, inverse_ref[...])
    for a in range(TRACE):
        out_ref[a] = robin[a : a + 1]


VMEM = pl.BlockSpec(memory_space=pltpu.VMEM)


HBM = pl.BlockSpec(memory_space=pl.ANY)


def call(kernel, name, outs, scratch, operands, in_hbm=0):
    return pl.pallas_call(
        kernel,
        name=name,
        out_shape=[jax.ShapeDtypeStruct(shape, dtype) for shape, dtype in outs],
        in_specs=[HBM] * in_hbm + [VMEM] * (len(operands) - in_hbm),
        out_specs=[VMEM] * len(outs),
        scratch_shapes=scratch,
        compiler_params=pltpu.CompilerParams(vmem_limit_bytes=16 << 20),
    )(*operands)


def pair_groups(groups, peers):
    return [[(2 * m + h) * peers + s for h in range(2) for s in range(peers)] for m in range(groups // 2)]


def partner_pairs(groups):
    pairs = []
    for odd in range(1, groups - 1, 2):
        pairs += [(odd, odd + 1), (odd + 1, odd)]
    return pairs


def body(
    load, couple, face_link, face_count, slot_face, pair_count, basis, coarse_inverse, coarse_block, coarse_link
):
    groups, peers = lax.axis_size("grp"), lax.axis_size("sub")
    blocks = pair_groups(groups, peers)
    partners = partner_pairs(groups)
    rows = 2 * peers

    def exchange(send):
        arrived = lax.all_to_all(
            send.reshape(rows, 1, LANES), ("grp", "sub"), 0, 0, axis_index_groups=blocks, tiled=True
        )
        return arrived.reshape(rows, LANES)

    integer = jnp.int32
    field = ((ROWS, FB), f32)
    sends = ((rows, LANES), f32)
    output = ((TRACE, 1, FB), f32)
    packed_shape = ((KC // 2 + 1) * CVEC + 8, LANES)
    work = [pltpu.VMEM((LINKS + 1, ROWS, FB), f32), pltpu.VMEM((ROWS, FB), f32)]
    face_links = jnp.moveaxis(face_link[0], 0, 1)
    couple_rows = jnp.swapaxes(couple[0, 0], 1, 2)
    basis_rows = jnp.swapaxes(basis[0, 0], 0, 1)
    given = [
        (face_count, pltpu.SMEM),
        (pair_count[0], pltpu.SMEM),
        (coarse_link[0], pltpu.SMEM),
        (slot_face[0, 0], pltpu.VMEM),
        (jnp.moveaxis(load[0], 0, 1), pltpu.VMEM),
        (face_links, pltpu.VMEM),
        (coarse_inverse[0, 0], pltpu.VMEM),
        (coarse_block[0, 0], pltpu.VMEM),
        (basis_rows, pltpu.VMEM),
    ]
    trace, source, live, inverse, wide_slots, mine, places, packed, start = call(
        functools.partial(first_kernel, groups, peers),
        "first",
        [
            field,
            field,
            ((1, FB), f32),
            ((1, FB), integer),
            ((peers, LANES), integer),
            ((8, LANES), integer),
            ((16, LANES), integer),
            (packed_shape, f32),
            sends,
        ],
        work + [space(x.shape, x.dtype) for x, space in given] + [pltpu.SemaphoreType.DMA((len(given),))],
        [given[0][0]]
        + [pltpu.with_memory_space_constraint(x, pltpu.HBM) for x, space in given[1:]]
        + [couple_rows],
        len(given),
    )
    robin = arrived = twin = None
    for outer_step in range(ITERS):
        first, last = outer_step == 0, outer_step == ITERS - 1
        if not first:
            trace, robin, start = call(
                local_kernel,
                "local",
                [field, field, sends],
                work,
                [arrived, live, inverse, source, face_links, packed, trace, couple_rows, basis_rows],
            )
        window = exchange(start)
        if first:
            twin = beyond = lax.ppermute(jnp.concatenate([window, packed], axis=0), "grp", partners)
        else:
            beyond = lax.ppermute(window, "grp", partners)
        (swept,) = call(sweep_kernel, "sweep", [sends], [], [places, window, beyond, packed, twin])
        swept = exchange(swept)
        operands = [places, live, mine, start, swept, packed, wide_slots, trace]
        operands += ([] if first else [robin]) + [basis_rows]
        results = call(
            functools.partial(correct_kernel, first, last),
            "correct",
            ([output, ((1, CVEC), f32)] if last else [field]) + [((peers * 8, LANES), f32)],
            [pltpu.VMEM((ROWS, FB), f32)],
            operands,
        )
        trace, outgoing = results[0], results[-1]
        if last:
            coefficients = results[1]
        arrived = lax.all_to_all(outgoing.reshape(peers, 8, LANES), "sub", 0, 0, tiled=True)
        arrived = arrived.reshape(peers * 8, LANES)
    (robin,) = call(robin_kernel, "robin", [output], [], [arrived, inverse])
    return (jnp.moveaxis(trace, 0, 1)[None], jnp.moveaxis(robin, 0, 1)[None], coefficients[None])


def solution(mesh):
    in_specs = (
        P("grp", "sub", None, None),
        P("grp", "sub", None, None, None, None),
        P("grp", "sub", None, None),
        P("grp", "sub"),
        P("grp", "sub", None, None),
        P("grp", "sub", None),
        P("grp", "sub", None, None, None),
        P("grp", "sub", None, None),
        P("grp", "sub", None, None, None),
        P("grp", "sub", None),
    )
    out_specs = (P("grp", "sub", None, None), P("grp", "sub", None, None), P("grp", "sub", None))
    return jax.shard_map(body, mesh=mesh, in_specs=in_specs, out_specs=out_specs, check_vma=False)
```

time: 173 us -> 145 us (0.84)
  the two profiles are of different devices: /device:TPU:1 before, /device:TPU:513 now
where the time goes in v2:
time: 145 us
  blocking collectives  108 us (74%)
  waiting for transfers between devices  13.9 us (10%)
  starting transfers between devices  11.6 us (8%)
  Pallas kernels  8.16 us (6%)
    all_to_all x6, blocking collectives, exchange(): lax.all_to_all(send.reshape(rows, 1, LANES), ('grp', 'sub'), 0, 0, axis_i...  75.4 us
    all_to_all x3, blocking collectives, body(): lax.all_to_all(outgoing.reshape(peers, 8, LANES), 'sub', 0, 0, tiled=True)  33 us
    ppermute x2, waiting for transfers between devices, body(): beyond = lax.ppermute(window, 'grp', partners)  8.72 us
    pallas_call x10, Pallas kernels, call(): pl.pallas_call(kernel, name=name, out_shape=[jax.ShapeDtypeStruct(shape,...  8.16 us
    ppermute x2, starting transfers between devices, body(): beyond = lax.ppermute(window, 'grp', partners)  6.85 us
    ppermute x1, waiting for transfers between devices, body(): lax.ppermute(jnp.concatenate([window, packed], axis=0), 'grp', partners)  5.19 us
    ppermute x1, starting transfers between devices, body(): lax.ppermute(jnp.concatenate([window, packed], axis=0), 'grp', partners)  4.7 us
  transfers between devices with their start and end apart: 3, of which 3 were waited for; matrix products, arithmetic and copies ran while one was open for 0% of the time, Pallas kernels for 0%

profile of v2, /device:TPU:513, one launch (start us, length us, event | category | flops | bytes accessed | tf_op | source)
XLA Modules:
  0.0 144.7 jit_solution(1485713463412004308)
XLA Ops:
  1.3 1.2 copy.26
  2.5 0.0 copy-start
  2.5 2.0 %first.1 = (f32[16,384]{1,0:T(8,128)S(1)}, f32[16,384]{1,0:T(8,128)S(1)}, f32[1,384]{1,0:T(1,128)S(1)}, s32[1,384]{1,0:T(1,128)S(1)}, s32[16,128]{1,0:T(8,128)S(...) custom-call(s32[1,1]{1,0:T(1,128)S(6)} %copy.27.count_hbm, ...), custom_call_target="tpu_custom_call" | custom-call | tf_op jit(solution)/shard_map/first/pallas_call | solution.py:350
  4.5 0.0 copy-start.1
  4.6 16.5 %all_to_all.45 = f32[32,1,128]{2,1,0:T(1,128)S(1)} all-to-all(f32[32,1,128]{2,1,0:T(1,128)S(1)} %bitcast.67), channel_id=1, replica_groups={{0,1,2,3,4,5,6,7,8,9,10,11,12,13,14,15,16,17,18,19,20,21,22,23,24,25,26..., dimensions={0} | all-to-all | bytes 32768 | tf_op jit(solution)/shard_map/all_to_all | solution.py:381
  21.1 4.7 %collective-permute-start = (f32[296,128]{1,0:T(8,128)S(1)}, f32[296,128]{1,0:T(8,128)S(1)}, u32[]{:S(2)}, u32[]{:S(2)}) collective-permute-start(f32[296,128]{1,0:T(8,128)S(1)} %pad_maximum_fusion), channel_id=1, source_target_pairs={{16,32},{32,16},{48,64},{64,48},{80,96},{96,80},{112,128},{128,112... | collective-permute-start | bytes 454664 | tf_op jit(solution)/shard_map/ppermute | solution.py:439
  25.8 5.2 %collective-permute-done.partner_ref.twin_ref = f32[296,128]{1,0:T(8,128)S(1)} collective-permute-done((f32[296,128]{1,0:T(8,128)S(1)}, f32[296,128]{1,0:T(8,128)S(1)}, u32[]{:S(2)}, u32[]{:S(2)}) %collective-permute-start) | collective-permute-done | bytes 151584 | tf_op jit(solution)/shard_map/ppermute | solution.py:439
  31.0 0.2 sweep.3
  31.2 12.3 %all_to_all.46 = f32[32,1,128]{2,1,0:T(1,128)S(1)} all-to-all(f32[32,1,128]{2,1,0:T(1,128)S(1)} %bitcast.81), channel_id=1, replica_groups={{0,1,2,3,4,5,6,7,8,9,10,11,12,13,14,15,16,17,18,19,20,21,22,23,24,25,26..., dimensions={0} | all-to-all | bytes 32768 | tf_op jit(solution)/shard_map/all_to_all | solution.py:381
  43.5 0.0 copy-done
  43.5 0.7 correct.3
  44.2 11.0 %all_to_all.47 = f32[16,8,128]{2,1,0:T(8,128)S(1)} all-to-all(f32[16,8,128]{2,1,0:T(8,128)S(1)} %bitcast.74), channel_id=1, replica_groups=mesh['grp'=48,'sub'=16] {'sub'}, dimensions={0} | all-to-all | bytes 131072 | tf_op jit(solution)/shard_map/all_to_all | solution.py:456
  55.2 0.0 copy-done.1
  55.2 1.2 local.2
  56.4 10.8 %all_to_all.48 = f32[32,1,128]{2,1,0:T(1,128)S(1)} all-to-all(f32[32,1,128]{2,1,0:T(1,128)S(1)} %bitcast.68), channel_id=1, replica_groups={{0,1,2,3,4,5,6,7,8,9,10,11,12,13,14,15,16,17,18,19,20,21,22,23,24,25,26..., dimensions={0} | all-to-all | bytes 32768 | tf_op jit(solution)/shard_map/all_to_all | solution.py:381
  67.1 3.9 %collective-permute-start.1 = (f32[32,128]{1,0:T(8,128)S(1)}, f32[32,128]{1,0:T(8,128)S(1)}, u32[]{:S(2)}, u32[]{:S(2)}) collective-permute-start(f32[32,128]{1,0:T(8,128)S(1)} %bitcast.77), channel_id=1, source_target_pairs={{16,32},{32,16},{48,64},{64,48},{80,96},{96,80},{112,128},{128,112... | collective-permute-start | bytes 49160 | tf_op jit(solution)/shard_map/ppermute | solution.py:441
  71.0 3.9 %collective-permute-done.1.partner_ref = f32[32,128]{1,0:T(8,128)S(1)} collective-permute-done((f32[32,128]{1,0:T(8,128)S(1)}, f32[32,128]{1,0:T(8,128)S(1)}, u32[]{:S(2)}, u32[]{:S(2)}) %collective-permute-start.1) | collective-permute-done | bytes 16416 | tf_op jit(solution)/shard_map/ppermute | solution.py:441
  74.9 0.2 sweep.4
  75.1 12.5 %all_to_all.49 = f32[32,1,128]{2,1,0:T(1,128)S(1)} all-to-all(f32[32,1,128]{2,1,0:T(1,128)S(1)} %bitcast.80), channel_id=1, replica_groups={{0,1,2,3,4,5,6,7,8,9,10,11,12,13,14,15,16,17,18,19,20,21,22,23,24,25,26..., dimensions={0} | all-to-all | bytes 32768 | tf_op jit(solution)/shard_map/all_to_all | solution.py:381
  87.7 0.7 correct.4
  88.4 11.0 %all_to_all.50 = f32[16,8,128]{2,1,0:T(8,128)S(1)} all-to-all(f32[16,8,128]{2,1,0:T(8,128)S(1)} %bitcast.73), channel_id=1, replica_groups=mesh['grp'=48,'sub'=16] {'sub'}, dimensions={0} | all-to-all | bytes 131072 | tf_op jit(solution)/shard_map/all_to_all | solution.py:456
  99.4 1.2 local.3
  100.6 10.8 %all_to_all.51 = f32[32,1,128]{2,1,0:T(1,128)S(1)} all-to-all(f32[32,1,128]{2,1,0:T(1,128)S(1)} %bitcast.66), channel_id=1, replica_groups={{0,1,2,3,4,5,6,7,8,9,10,11,12,13,14,15,16,17,18,19,20,21,22,23,24,25,26..., dimensions={0} | all-to-all | bytes 32768 | tf_op jit(solution)/shard_map/all_to_all | solution.py:381
  111.4 3.0 %collective-permute-start.2 = (f32[32,128]{1,0:T(8,128)S(1)}, f32[32,128]{1,0:T(8,128)S(1)}, u32[]{:S(2)}, u32[]{:S(2)}) collective-permute-start(f32[32,128]{1,0:T(8,128)S(1)} %bitcast.75), channel_id=1, source_target_pairs={{16,32},{32,16},{48,64},{64,48},{80,96},{96,80},{112,128},{128,112... | collective-permute-start | bytes 49160 | tf_op jit(solution)/shard_map/ppermute | solution.py:441
  114.3 4.8 %collective-permute-done.2.partner_ref = f32[32,128]{1,0:T(8,128)S(1)} collective-permute-done((f32[32,128]{1,0:T(8,128)S(1)}, f32[32,128]{1,0:T(8,128)S(1)}, u32[]{:S(2)}, u32[]{:S(2)}) %collective-permute-start.2) | collective-permute-done | bytes 16416 | tf_op jit(solution)/shard_map/ppermute | solution.py:441
  119.1 0.2 sweep.5
  119.4 12.5 %all_to_all.52 = f32[32,1,128]{2,1,0:T(1,128)S(1)} all-to-all(f32[32,1,128]{2,1,0:T(1,128)S(1)} %bitcast.79), channel_id=1, replica_groups={{0,1,2,3,4,5,6,7,8,9,10,11,12,13,14,15,16,17,18,19,20,21,22,23,24,25,26..., dimensions={0} | all-to-all | bytes 32768 | tf_op jit(solution)/shard_map/all_to_all | solution.py:381
  131.9 1.0 correct.5
  132.9 11.0 %all_to_all.53 = f32[16,8,128]{2,1,0:T(8,128)S(1)} all-to-all(f32[16,8,128]{2,1,0:T(8,128)S(1)} %bitcast.72), channel_id=1, replica_groups=mesh['grp'=48,'sub'=16] {'sub'}, dimensions={0} | all-to-all | bytes 131072 | tf_op jit(solution)/shard_map/all_to_all | solution.py:456
  143.9 0.7 robin.1
  (1 shorter events, 0.0 us)
Async XLA Ops:
  2.5 41.0 %copy-start = (f32[1,1,64,15,384]{4,2,3,1,0:T(8,128)S(1)}, f32[1,1,64,15,384]{4,2,3,1,0:T(8,128)}, u32[]{:S(2)}) copy-start(f32[1,1,64,15,384]{4,2,3,1,0:T(8,128)} %param.16) | copy-start | bytes 4423684
  4.5 50.6 %copy-start.1 = (s32[1,1,3,384]{3,1,2,0:T(1,128)S(1)}, s32[1,1,3,384]{3,1,2,0:T(1,128)}, u32[]{:S(2)}) copy-start(s32[1,1,3,384]{3,1,2,0:T(1,128)} %param.12) | copy-start | bytes 13828
  21.1 9.9 %collective-permute-start = (f32[296,128]{1,0:T(8,128)S(1)}, f32[296,128]{1,0:T(8,128)S(1)}, u32[]{:S(2)}, u32[]{:S(2)}) collective-permute-start(f32[296,128]{1,0:T(8,128)S(1)} %pad_maximum_fusion), channel_id=1, source_target_pairs={{16,32},{32,16},{48,64},{64,48},{80,96},{96,80},{112,128},{128,112... | collective-permute-start | bytes 454664 | tf_op jit(solution)/shard_map/ppermute | solution.py:439
  67.1 7.8 %collective-permute-start.1 = (f32[32,128]{1,0:T(8,128)S(1)}, f32[32,128]{1,0:T(8,128)S(1)}, u32[]{:S(2)}, u32[]{:S(2)}) collective-permute-start(f32[32,128]{1,0:T(8,128)S(1)} %bitcast.77), channel_id=1, source_target_pairs={{16,32},{32,16},{48,64},{64,48},{80,96},{96,80},{112,128},{128,112... | collective-permute-start | bytes 49160 | tf_op jit(solution)/shard_map/ppermute | solution.py:441
  111.4 7.8 %collective-permute-start.2 = (f32[32,128]{1,0:T(8,128)S(1)}, f32[32,128]{1,0:T(8,128)S(1)}, u32[]{:S(2)}, u32[]{:S(2)}) collective-permute-start(f32[32,128]{1,0:T(8,128)S(1)} %bitcast.75), channel_id=1, source_target_pairs={{16,32},{32,16},{48,64},{64,48},{80,96},{96,80},{112,128},{128,112... | collective-permute-start | bytes 49160 | tf_op jit(solution)/shard_map/ppermute | solution.py:441

commit v3 on v2

--- a/solution.py
+++ b/solution.py
@@ -119,7 +119,7 @@
     return jnp.where(inverse_row >= 0, rows, 0.0)
 
 
-def start_coarse(blocks_ref, basis_ref, residual, rows_ref, send_ref):
+def start_coarse(matrix_ref, basis_ref, residual, rows_ref, send_ref):
     rows_ref[:TRACE, :] = residual
     totals = [None] * (FB // LANES)
     for a in range(TRACE):
@@ -128,7 +128,7 @@
             term = basis_ref[a, :, lanes] * rows_ref[a : a + 1, lanes]
             totals[t] = term if totals[t] is None else totals[t] + term
     restricted = jnp.sum(totals[0] + totals[1] + totals[2], axis=1, keepdims=True)
-    start = jnp.sum(blocks_ref[:CVEC, :] * as_row(restricted), axis=1, keepdims=True)
+    start = jnp.sum(matrix_ref[...] * as_row(restricted)[:, :CVEC], axis=1, keepdims=True)
     send_ref[...] = jnp.broadcast_to(as_row(start, start), send_ref.shape)
 
 
@@ -233,7 +233,7 @@
         spots = list(zip(spots[0::2], spots[1::2])) + [(place(myself, pair, other),) * 2]
         index = place_rows(spots)
         if at:
-            blocks_ref[(KC // 2 + 1) * CVEC :, :] = index.astype(f32)
+            blocks_ref[KC // 2 * CVEC :, :] = index.astype(f32)
         else:
             places_ref[:8, :] = index
     spots = []
@@ -244,15 +244,18 @@
 
     for move in moves[6:]:
         move.wait()
-    blocks_ref[:CVEC, :] = jnp.concatenate([matrix_ref[...], jnp.zeros((CVEC, CVEC), f32)], axis=1)
+    matrix = matrix_ref[...]
     for k in range(0, KC, 2):
-        at = (k // 2 + 1) * CVEC
-        blocks_ref[at : at + CVEC, :] = jnp.concatenate([coupling_ref[k], coupling_ref[k + 1]], axis=1)
-    start_coarse(blocks_ref, basis_ref, residual, rows_ref, send_ref)
+        at = k // 2 * CVEC
+        pair = jnp.concatenate([coupling_ref[k], coupling_ref[k + 1]], axis=1)
+        blocks_ref[at : at + CVEC, :] = jnp.dot(
+            matrix, pair, precision=lax.Precision.HIGHEST, preferred_element_type=f32
+        )
+    start_coarse(matrix_ref, basis_ref, residual, rows_ref, send_ref)
 
 
 def local_kernel(
-    arrived_ref, live_ref, inverse_ref, load_ref, link_ref, blocks_ref, old_ref, couple_ref, basis_ref,
+    arrived_ref, live_ref, inverse_ref, load_ref, link_ref, matrix_ref, old_ref, couple_ref, basis_ref,
     trace_ref, robin_ref, send_ref,
     stack_ref, rows_ref,
 ):
@@ -267,24 +270,23 @@
     )
     trace_ref[...] = robin
     trace_ref[:TRACE, :] = trace
-    start_coarse(blocks_ref, basis_ref, residual, rows_ref, send_ref)
+    start_coarse(matrix_ref, basis_ref, residual, rows_ref, send_ref)
 
 
 def coarse_step(blocks_ref, first, pair_rows):
     total = None
     for k in range(KC // 2):
-        matrix = blocks_ref[first + (k + 1) * CVEC : first + (k + 2) * CVEC, :]
+        matrix = blocks_ref[first + k * CVEC : first + (k + 1) * CVEC, :]
         term = matrix * pair_rows[k : k + 1]
         total = term if total is None else total + term
-    coupled = jnp.sum(total, axis=1, keepdims=True)
-    return jnp.sum(blocks_ref[first : first + CVEC, :] * as_row(coupled), axis=1, keepdims=True)
+    return jnp.sum(total, axis=1, keepdims=True)
 
 
 def sweep_kernel(places_ref, own_ref, partner_ref, blocks_ref, twin_ref, send_ref):
     rows = own_ref.shape[0]
     window = blocks_of(own_ref, rows) + blocks_of(partner_ref, rows)
     own = pick_rows(window, places_ref[:8, :])
-    after = rows + (KC // 2 + 1) * CVEC
+    after = rows + KC // 2 * CVEC
     twin = pick_rows(window, twin_ref[after : after + 8, :].astype(jnp.int32))
     steps = [coarse_step(blocks_ref, 0, own), coarse_step(twin_ref, rows, twin)]
     at = KC // 2
@@ -318,11 +320,7 @@
             rows_ref[a : a + 1, lanes] = jnp.sum(basis_ref[a, :, lanes] * spread, axis=0, keepdims=True)
     rows_ref[TRACE:, :] = jnp.zeros((ROWS - TRACE, FB), f32)
     trace = trace_ref[...] + live * rows_ref[...]
-    if last:
-        for a in range(TRACE):
-            out_ref[a] = trace[a : a + 1]
-    else:
-        out_ref[...] = trace
+    out_ref[...] = trace
     outgoing = 2.0 * robin_weight * trace
     if not first:
         outgoing = outgoing - robin_ref[...]
@@ -334,10 +332,21 @@
         packed_ref[j * 8 : (j + 1) * 8, :] = jnp.where(mine, pick(upper, index), pick(lower, index))
 
 
-def robin_kernel(arrived_ref, inverse_ref, out_ref):
-    robin = unpack_slots(arrived_ref, inverse_ref[...])
-    for a in range(TRACE):
-        out_ref[a] = robin[a : a + 1]
+def robin_kernel(
+    trace_ref, arrived_ref, inverse_ref, trace_hbm, robin_hbm, trace_rows, robin_rows, sems
+):
+    moves = []
+
+    def put(values, rows_ref, target):
+        for a in range(TRACE):
+            rows_ref[a] = values[a : a + 1]
+        moves.append(pltpu.make_async_copy(rows_ref, target, sems.at[len(moves)]))
+        moves[-1].start()
+
+    put(trace_ref[...], trace_rows, trace_hbm)
+    put(unpack_slots(arrived_ref, inverse_ref[...]), robin_rows, robin_hbm)
+    for move in moves:
+        move.wait()
 
 
 VMEM = pl.BlockSpec(memory_space=pltpu.VMEM)
@@ -346,13 +355,13 @@
 HBM = pl.BlockSpec(memory_space=pl.ANY)
 
 
-def call(kernel, name, outs, scratch, operands, in_hbm=0):
+def call(kernel, name, outs, scratch, operands, in_hbm=0, out_hbm=0):
     return pl.pallas_call(
         kernel,
         name=name,
         out_shape=[jax.ShapeDtypeStruct(shape, dtype) for shape, dtype in outs],
         in_specs=[HBM] * in_hbm + [VMEM] * (len(operands) - in_hbm),
-        out_specs=[VMEM] * len(outs),
+        out_specs=[HBM] * out_hbm + [VMEM] * (len(outs) - out_hbm),
         scratch_shapes=scratch,
         compiler_params=pltpu.CompilerParams(vmem_limit_bytes=16 << 20),
     )(*operands)
@@ -387,10 +396,10 @@
     field = ((ROWS, FB), f32)
     sends = ((rows, LANES), f32)
     output = ((TRACE, 1, FB), f32)
-    packed_shape = ((KC // 2 + 1) * CVEC + 8, LANES)
+    packed_shape = (KC // 2 * CVEC + 8, LANES)
     work = [pltpu.VMEM((LINKS + 1, ROWS, FB), f32), pltpu.VMEM((ROWS, FB), f32)]
     face_links = jnp.moveaxis(face_link[0], 0, 1)
-    couple_rows = jnp.swapaxes(couple[0, 0], 1, 2)
+    couple_rows = jnp.swapaxes(couple[0, 0], 1, 2).astype(f32)
     basis_rows = jnp.swapaxes(basis[0, 0], 0, 1)
     given = [
         (face_count, pltpu.SMEM),
@@ -432,7 +441,9 @@
                 "local",
                 [field, field, sends],
                 work,
-                [arrived, live, inverse, source, face_links, packed, trace, couple_rows, basis_rows],
+                [
+                    arrived, live, inverse, source, face_links, coarse_inverse[0, 0], trace, couple_rows, basis_rows
+                ],
             )
         window = exchange(start)
         if first:
@@ -446,7 +457,7 @@
         results = call(
             functools.partial(correct_kernel, first, last),
             "correct",
-            ([output, ((1, CVEC), f32)] if last else [field]) + [((peers * 8, LANES), f32)],
+            [field] + ([((1, CVEC), f32)] if last else []) + [((peers * 8, LANES), f32)],
             [pltpu.VMEM((ROWS, FB), f32)],
             operands,
         )
@@ -455,7 +466,14 @@
             coefficients = results[1]
         arrived = lax.all_to_all(outgoing.reshape(peers, 8, LANES), "sub", 0, 0, tiled=True)
         arrived = arrived.reshape(peers * 8, LANES)
-    (robin,) = call(robin_kernel, "robin", [output], [], [arrived, inverse])
+    trace, robin = call(
+        robin_kernel,
+        "robin",
+        [output, output],
+        [pltpu.VMEM(*output), pltpu.VMEM(*output), pltpu.SemaphoreType.DMA((2,))],
+        [trace, arrived, inverse],
+        out_hbm=2,
+    )
     return (jnp.moveaxis(trace, 0, 1)[None], jnp.moveaxis(robin, 0, 1)[None], coefficients[None])
 
 

time: 145 us -> 144 us (level)
  no operation moved by 1% of the time
where the time goes in v3:
time: 144 us; the launch traced here: 143 us
  blocking collectives  109 us (76%)
  waiting for transfers between devices  12.9 us (9%)
  starting transfers between devices  11.6 us (8%)
  Pallas kernels  7.26 us (5%)
    all_to_all x6, blocking collectives, exchange(): lax.all_to_all(send.reshape(rows, 1, LANES), ('grp', 'sub'), 0, 0, axis_i...  75.7 us
    all_to_all x3, blocking collectives, body(): lax.all_to_all(outgoing.reshape(peers, 8, LANES), 'sub', 0, 0, tiled=True)  33 us
    ppermute x2, waiting for transfers between devices, body(): beyond = lax.ppermute(window, 'grp', partners)  8.72 us
    pallas_call x10, Pallas kernels, call(): pl.pallas_call(kernel, name=name, out_shape=[jax.ShapeDtypeStruct(shape,...  7.26 us
    ppermute x2, starting transfers between devices, body(): beyond = lax.ppermute(window, 'grp', partners)  6.85 us
    ppermute x1, starting transfers between devices, body(): lax.ppermute(jnp.concatenate([window, packed], axis=0), 'grp', partners)  4.7 us
    ppermute x1, waiting for transfers between devices, body(): lax.ppermute(jnp.concatenate([window, packed], axis=0), 'grp', partners)  4.19 us
  transfers between devices with their start and end apart: 3, of which 3 were waited for; matrix products, arithmetic and copies ran while one was open for 0% of the time, Pallas kernels for 0%

profile of v3, /device:TPU:513, one launch (start us, length us, event | category | flops | bytes accessed | tf_op | source)
XLA Modules:
  0.0 143.1 jit_solution(11585670663027785734)
XLA Ops:
  1.3 1.2 convert_bitcast_fusion.couple_ref
  2.5 0.0 copy-start
  2.5 2.1 %first.1 = (f32[16,384]{1,0:T(8,128)S(1)}, f32[16,384]{1,0:T(8,128)S(1)}, f32[1,384]{1,0:T(1,128)S(1)}, s32[1,384]{1,0:T(1,128)S(1)}, s32[16,128]{1,0:T(8,128)S(...) custom-call(s32[1,1]{1,0:T(1,128)S(6)} %copy.26.count_hbm, ...), custom_call_target="tpu_custom_call" | custom-call | tf_op jit(solution)/shard_map/first/pallas_call | solution.py:359
  4.6 0.0 copy-start.1
  4.6 0.0 copy-start.2
  4.6 16.5 %all_to_all.45 = f32[32,1,128]{2,1,0:T(1,128)S(1)} all-to-all(f32[32,1,128]{2,1,0:T(1,128)S(1)} %bitcast.67), channel_id=1, replica_groups={{0,1,2,3,4,5,6,7,8,9,10,11,12,13,14,15,16,17,18,19,20,21,22,23,24,25,26..., dimensions={0} | all-to-all | bytes 32768 | tf_op jit(solution)/shard_map/all_to_all | solution.py:390
  21.1 4.7 %collective-permute-start = (f32[232,128]{1,0:T(8,128)S(1)}, f32[232,128]{1,0:T(8,128)S(1)}, u32[]{:S(2)}, u32[]{:S(2)}) collective-permute-start(f32[232,128]{1,0:T(8,128)S(1)} %pad_maximum_fusion), channel_id=1, source_target_pairs={{16,32},{32,16},{48,64},{64,48},{80,96},{96,80},{112,128},{128,112... | collective-permute-start | bytes 356360 | tf_op jit(solution)/shard_map/ppermute | solution.py:450
  25.8 4.2 %collective-permute-done.partner_ref.twin_ref = f32[232,128]{1,0:T(8,128)S(1)} collective-permute-done((f32[232,128]{1,0:T(8,128)S(1)}, f32[232,128]{1,0:T(8,128)S(1)}, u32[]{:S(2)}, u32[]{:S(2)}) %collective-permute-start) | collective-permute-done | bytes 118816 | tf_op jit(solution)/shard_map/ppermute | solution.py:450
  30.0 0.1 sweep.3
  30.2 12.6 %all_to_all.46 = f32[32,1,128]{2,1,0:T(1,128)S(1)} all-to-all(f32[32,1,128]{2,1,0:T(1,128)S(1)} %bitcast.78), channel_id=1, replica_groups={{0,1,2,3,4,5,6,7,8,9,10,11,12,13,14,15,16,17,18,19,20,21,22,23,24,25,26..., dimensions={0} | all-to-all | bytes 32768 | tf_op jit(solution)/shard_map/all_to_all | solution.py:390
  42.7 0.0 copy-done
  42.7 0.6 correct.3
  43.3 11.0 %all_to_all.47 = f32[16,8,128]{2,1,0:T(8,128)S(1)} all-to-all(f32[16,8,128]{2,1,0:T(8,128)S(1)} %bitcast.81), channel_id=1, replica_groups=mesh['grp'=48,'sub'=16] {'sub'}, dimensions={0} | all-to-all | bytes 131072 | tf_op jit(solution)/shard_map/all_to_all | solution.py:467
  54.3 0.0 copy-done.1
  54.3 0.0 copy-done.2
  54.3 1.0 local.2
  55.4 10.8 %all_to_all.48 = f32[32,1,128]{2,1,0:T(1,128)S(1)} all-to-all(f32[32,1,128]{2,1,0:T(1,128)S(1)} %bitcast.68), channel_id=1, replica_groups={{0,1,2,3,4,5,6,7,8,9,10,11,12,13,14,15,16,17,18,19,20,21,22,23,24,25,26..., dimensions={0} | all-to-all | bytes 32768 | tf_op jit(solution)/shard_map/all_to_all | solution.py:390
  66.1 3.9 %collective-permute-start.1 = (f32[32,128]{1,0:T(8,128)S(1)}, f32[32,128]{1,0:T(8,128)S(1)}, u32[]{:S(2)}, u32[]{:S(2)}) collective-permute-start(f32[32,128]{1,0:T(8,128)S(1)} %bitcast.74), channel_id=1, source_target_pairs={{16,32},{32,16},{48,64},{64,48},{80,96},{96,80},{112,128},{128,112... | collective-permute-start | bytes 49160 | tf_op jit(solution)/shard_map/ppermute | solution.py:452
  70.0 3.9 %collective-permute-done.1.partner_ref = f32[32,128]{1,0:T(8,128)S(1)} collective-permute-done((f32[32,128]{1,0:T(8,128)S(1)}, f32[32,128]{1,0:T(8,128)S(1)}, u32[]{:S(2)}, u32[]{:S(2)}) %collective-permute-start.1) | collective-permute-done | bytes 16416 | tf_op jit(solution)/shard_map/ppermute | solution.py:452
  73.9 0.1 sweep.4
  74.0 12.5 %all_to_all.49 = f32[32,1,128]{2,1,0:T(1,128)S(1)} all-to-all(f32[32,1,128]{2,1,0:T(1,128)S(1)} %bitcast.77), channel_id=1, replica_groups={{0,1,2,3,4,5,6,7,8,9,10,11,12,13,14,15,16,17,18,19,20,21,22,23,24,25,26..., dimensions={0} | all-to-all | bytes 32768 | tf_op jit(solution)/shard_map/all_to_all | solution.py:390
  86.6 0.6 correct.4
  87.2 11.0 %all_to_all.50 = f32[16,8,128]{2,1,0:T(8,128)S(1)} all-to-all(f32[16,8,128]{2,1,0:T(8,128)S(1)} %bitcast.80), channel_id=1, replica_groups=mesh['grp'=48,'sub'=16] {'sub'}, dimensions={0} | all-to-all | bytes 131072 | tf_op jit(solution)/shard_map/all_to_all | solution.py:467
  98.2 1.0 local.3
  99.2 10.8 %all_to_all.51 = f32[32,1,128]{2,1,0:T(1,128)S(1)} all-to-all(f32[32,1,128]{2,1,0:T(1,128)S(1)} %bitcast.66), channel_id=1, replica_groups={{0,1,2,3,4,5,6,7,8,9,10,11,12,13,14,15,16,17,18,19,20,21,22,23,24,25,26..., dimensions={0} | all-to-all | bytes 32768 | tf_op jit(solution)/shard_map/all_to_all | solution.py:390
  110.0 3.0 %collective-permute-start.2 = (f32[32,128]{1,0:T(8,128)S(1)}, f32[32,128]{1,0:T(8,128)S(1)}, u32[]{:S(2)}, u32[]{:S(2)}) collective-permute-start(f32[32,128]{1,0:T(8,128)S(1)} %bitcast.72), channel_id=1, source_target_pairs={{16,32},{32,16},{48,64},{64,48},{80,96},{96,80},{112,128},{128,112... | collective-permute-start | bytes 49160 | tf_op jit(solution)/shard_map/ppermute | solution.py:452
  113.0 4.8 %collective-permute-done.2.partner_ref = f32[32,128]{1,0:T(8,128)S(1)} collective-permute-done((f32[32,128]{1,0:T(8,128)S(1)}, f32[32,128]{1,0:T(8,128)S(1)}, u32[]{:S(2)}, u32[]{:S(2)}) %collective-permute-start.2) | collective-permute-done | bytes 16416 | tf_op jit(solution)/shard_map/ppermute | solution.py:452
  117.8 0.1 sweep.5
  117.9 12.5 %all_to_all.52 = f32[32,1,128]{2,1,0:T(1,128)S(1)} all-to-all(f32[32,1,128]{2,1,0:T(1,128)S(1)} %bitcast.76), channel_id=1, replica_groups={{0,1,2,3,4,5,6,7,8,9,10,11,12,13,14,15,16,17,18,19,20,21,22,23,24,25,26..., dimensions={0} | all-to-all | bytes 32768 | tf_op jit(solution)/shard_map/all_to_all | solution.py:390
  130.4 0.9 correct.5
  131.3 11.0 %all_to_all.53 = f32[16,8,128]{2,1,0:T(8,128)S(1)} all-to-all(f32[16,8,128]{2,1,0:T(8,128)S(1)} %bitcast.79), channel_id=1, replica_groups=mesh['grp'=48,'sub'=16] {'sub'}, dimensions={0} | all-to-all | bytes 131072 | tf_op jit(solution)/shard_map/all_to_all | solution.py:467
  142.3 0.8 robin.1
  (1 shorter events, 0.0 us)
Async XLA Ops:
  2.5 40.2 %copy-start = (f32[1,1,64,15,384]{4,2,3,1,0:T(8,128)S(1)}, f32[1,1,64,15,384]{4,2,3,1,0:T(8,128)}, u32[]{:S(2)}) copy-start(f32[1,1,64,15,384]{4,2,3,1,0:T(8,128)} %param.16) | copy-start | bytes 4423684
  4.6 49.7 %copy-start.1 = (f32[1,1,64,64]{3,2,1,0:T(8,128)S(1)}, f32[1,1,64,64]{3,2,1,0:T(8,128)}, u32[]{:S(2)}) copy-start(f32[1,1,64,64]{3,2,1,0:T(8,128)} %param.17) | copy-start | bytes 49156
  4.6 49.7 %copy-start.2 = (s32[1,1,3,384]{3,1,2,0:T(1,128)S(1)}, s32[1,1,3,384]{3,1,2,0:T(1,128)}, u32[]{:S(2)}) copy-start(s32[1,1,3,384]{3,1,2,0:T(1,128)} %param.12) | copy-start | bytes 13828
  21.1 8.9 %collective-permute-start = (f32[232,128]{1,0:T(8,128)S(1)}, f32[232,128]{1,0:T(8,128)S(1)}, u32[]{:S(2)}, u32[]{:S(2)}) collective-permute-start(f32[232,128]{1,0:T(8,128)S(1)} %pad_maximum_fusion), channel_id=1, source_target_pairs={{16,32},{32,16},{48,64},{64,48},{80,96},{96,80},{112,128},{128,112... | collective-permute-start | bytes 356360 | tf_op jit(solution)/shard_map/ppermute | solution.py:450
  66.1 7.8 %collective-permute-start.1 = (f32[32,128]{1,0:T(8,128)S(1)}, f32[32,128]{1,0:T(8,128)S(1)}, u32[]{:S(2)}, u32[]{:S(2)}) collective-permute-start(f32[32,128]{1,0:T(8,128)S(1)} %bitcast.74), channel_id=1, source_target_pairs={{16,32},{32,16},{48,64},{64,48},{80,96},{96,80},{112,128},{128,112... | collective-permute-start | bytes 49160 | tf_op jit(solution)/shard_map/ppermute | solution.py:452
  110.0 7.8 %collective-permute-start.2 = (f32[32,128]{1,0:T(8,128)S(1)}, f32[32,128]{1,0:T(8,128)S(1)}, u32[]{:S(2)}, u32[]{:S(2)}) collective-permute-start(f32[32,128]{1,0:T(8,128)S(1)} %bitcast.72), channel_id=1, source_target_pairs={{16,32},{32,16},{48,64},{64,48},{80,96},{96,80},{112,128},{128,112... | collective-permute-start | bytes 49160 | tf_op jit(solution)/shard_map/ppermute | solution.py:452
